TPU v7x, 32 devices: a whole 2x2x4 slice. The times are simulated.
32 devices in a mesh: grp: 2 (over x), gz: 16 (over z, y, core).
Axes of the slice: x: 2, y: 2, z: 4, core: 2. Of those that a mesh axis runs over, the one named last changes fastest.
Arguments:
- features: bfloat16 [12, 128, 32, 128], P(None, ('grp', 'gz')), parts along dimension 1, may hold values from -6 to 6
- w_first: bfloat16 [48, 324], replicated, may hold values from -0.5 to 0.5
- w_second: bfloat16 [96, 1296], replicated, may hold values from -0.25 to 0.25
- w_lift: bfloat16 [48, 96], replicated, may hold values from -0.875 to 0.875
- w_merge: bfloat16 [12, 1296], replicated, may hold values from -0.15625 to 0.15625
- w_affine: bfloat16 [3, 12], replicated, may hold values from -2.5 to 2.5
- tissue: int32 [32, 32], P(('grp', 'gz')), parts along dimension 0, may hold values from 0 to 31
- owners: int32 [32, 32], P(('grp', 'gz')), parts along dimension 0, may hold values from 0 to 15, as said below
Outputs:
- routed: bfloat16 [32, 16, 2, 1536], P(('grp', 'gz')), parts along dimension 0
There are 2 independent parts, one for each index of `grp`. A program takes and returns all parts, laid end to end along the dimension named above; an argument that names none is the same for every part. Nothing has to cross between parts.
Inputs may be any that keep to these rules, and one draw needn't show every extreme that they name: `owners`: A device sends at most 2 of its listed blocks to one owner; in every draw some owner receives exactly 2 from every device.
All inputs are finite; a program needn't handle non-finite values.
Results may differ from a plain program's by a relative error of at most 0.0054.
Values may be sent and summed in bfloat16 or wider, within the bound.
No kernel may reach another device: no remote copies, remote signals or barrier semaphores. Data moves between devices by JAX's collectives and lax.ppermute only.
A program may use at most 128 MiB of HBM per device.

v0:
```python
import jax
import jax.numpy as jnp
from jax import lax
from jax.sharding import PartitionSpec as P

BY = 8
BX = 16
SEND_CAP = 2


def padded_2(cells, sides, width):
    for axis, dim in sides:
        count = lax.axis_size(axis)
        ends = count - 1
        head = lax.slice_in_dim(cells, 0, width, axis=dim)
        tail = lax.slice_in_dim(cells, cells.shape[dim] - width, cells.shape[dim], axis=dim)
        cells = jnp.concatenate(
            [
                lax.ppermute(tail, axis, [(i, (i + 1) % count) for i in range(ends)]),
                cells,
                lax.ppermute(head, axis, [((i + 1) % count, i) for i in range(ends)]),
            ],
            axis=dim,
        )
    return cells


def plane_terms(padded_plane, weight_slab):
    channels = padded_plane.shape[0]
    rows = padded_plane.shape[1] - 2
    columns = padded_plane.shape[2] - 2
    summed = jnp.zeros((weight_slab.shape[0], rows, columns), jnp.float32)
    for offset_y in range(3):
        stacked = jnp.concatenate(
            [
                padded_plane[:, offset_y : offset_y + rows, offset_x : offset_x + columns]
                for offset_x in range(3)
            ],
            axis=0,
        )
        weight_part = weight_slab[:, offset_y * 3 * channels : (offset_y + 1) * 3 * channels]
        summed = summed + jnp.einsum(
            "oi,iyx->oyx", weight_part, stacked, preferred_element_type=jnp.float32
        )
    return summed


def convolve(volume, weight, depth_pad):
    padded = jnp.pad(volume, ((0, 0), (depth_pad, depth_pad), (1, 1), (1, 1)))
    out_depth = padded.shape[1] - 2
    channels = volume.shape[0]

    def one_plane(plane_at):
        window_planes = lax.dynamic_slice_in_dim(padded, plane_at, 3, 1)
        summed = plane_terms(window_planes[:, 0], weight[:, 0 : 9 * channels])
        summed = summed + plane_terms(window_planes[:, 1], weight[:, 9 * channels : 18 * channels])
        summed = summed + plane_terms(window_planes[:, 2], weight[:, 18 * channels : 27 * channels])
        return summed

    planes = lax.map(one_plane, jnp.arange(out_depth, dtype=jnp.int32))
    return planes.transpose(1, 0, 2, 3)


def pad_plane(plane):
    return jnp.pad(plane, ((0, 0), (1, 1), (1, 1)))


def maxpool(volume):
    shape = volume.shape
    return volume.reshape(shape[0], shape[1] // 2, 2, shape[2] // 2, 2, shape[3] // 2, 2).max(
        axis=(2, 4, 6)
    )


def upsample(volume):
    shape = volume.shape
    spread = jnp.broadcast_to(
        volume[:, :, None, :, None, :, None], (shape[0], shape[1], 2, shape[2], 2, shape[3], 2)
    )
    return spread.reshape(shape[0], 2 * shape[1], 2 * shape[2], 2 * shape[3])


def on_device(features, w_first, w_second, w_lift, w_merge, w_affine, tissue, owners):
    depth = features.shape[1]
    widened = padded_2(features, (("gz", 1),), 1)
    first_map = jax.nn.relu(convolve(widened, w_first, 0)).astype(jnp.bfloat16)
    pooled_wide = padded_2(maxpool(first_map), (("gz", 1),), 1)
    second_map = jax.nn.relu(convolve(pooled_wide, w_second, 0)).astype(jnp.bfloat16)
    lifted = jnp.einsum("oc,czyx->ozyx", w_lift, second_map, preferred_element_type=jnp.float32)
    merged = (upsample(lifted) + first_map.astype(jnp.float32)).astype(jnp.bfloat16)
    inner = convolve(merged, w_merge, 1)
    channels = merged.shape[0]
    upward = plane_terms(pad_plane(merged[:, depth - 1]), w_merge[:, 0 : 9 * channels])[:, None]
    downward = plane_terms(pad_plane(merged[:, 0]), w_merge[:, 18 * channels : 27 * channels])[
        :, None
    ]
    edges = padded_2(
        jnp.concatenate([downward, upward], axis=1).astype(jnp.bfloat16), (("gz", 1),), 1
    ).astype(jnp.float32)
    lower_term = edges[:, :1]
    upper_term = edges[:, 3:]
    third_map = jnp.concatenate(
        [inner[:, :1] + lower_term, inner[:, 1 : depth - 1], inner[:, depth - 1 :] + upper_term],
        axis=1,
    )
    third_map = jax.nn.relu(third_map)
    affinity = jax.nn.sigmoid(
        jnp.einsum(
            "ac,czyx->azyx",
            w_affine.astype(jnp.float32),
            third_map,
            precision=lax.Precision.HIGHEST,
        )
    ).astype(jnp.bfloat16)
    shape = affinity.shape
    block_rows = shape[2] // BY
    block_cols = shape[3] // BX
    tiles = (
        affinity.reshape(shape[0], shape[1], block_rows, BY, block_cols, BX)
        .transpose(2, 4, 0, 1, 3, 5)
        .reshape(block_rows * block_cols, -1)
    )
    listed = tissue[0]
    owner_row = owners[0]
    count = listed.shape[0]
    devices = lax.axis_size("gz")
    slot_total = SEND_CAP * devices
    same_owner = owner_row[:, None] == owner_row[None, :]
    earlier = jnp.arange(count)[None, :] < jnp.arange(count)[:, None]
    ranks = jnp.sum(same_owner & earlier, axis=1)
    slot_index = owner_row * SEND_CAP + ranks
    slot_pick = (slot_index[:, None] == jnp.arange(slot_total, dtype=jnp.int32)[None, :]).astype(
        jnp.bfloat16
    )
    block_pick = (listed[:, None] == jnp.arange(tiles.shape[0], dtype=jnp.int32)[None, :]).astype(
        jnp.bfloat16
    )
    select = jnp.dot(slot_pick.T, block_pick, preferred_element_type=jnp.float32).astype(
        jnp.bfloat16
    )
    outgoing = jnp.dot(select, tiles, preferred_element_type=jnp.float32).astype(jnp.bfloat16)
    outgoing = outgoing.reshape(devices, SEND_CAP, tiles.shape[1])
    received = lax.all_to_all(outgoing, "gz", split_axis=0, concat_axis=0, tiled=True)
    return received[None]


def solution(mesh):
    placed = (
        P(None, ("grp", "gz"), None, None),
        P(),
        P(),
        P(),
        P(),
        P(),
        P(("grp", "gz"), None),
        P(("grp", "gz"), None),
    )
    return jax.shard_map(
        on_device,
        mesh=mesh,
        in_specs=placed,
        out_specs=P(("grp", "gz"), None, None, None),
        check_vma=False,
    )
```

profile of v0, /device:TPU:0, one launch (start us, length us, event | category | flops | bytes accessed | tf_op | source)
XLA Modules:
  0.0 166.6 jit_solution(14068969063575705335)
XLA Ops:
  0.0 1.3 copy.24
  1.3 2.4 %collective-permute-start = (bf16[12,1,32,128]{3,0,2,1:T(8,128)(2,1)S(1)}, bf16[12,1,32,128]{3,0,2,1:T(8,128)(2,1)S(1)}, u32[]{:S(2)}, u32[]{:S(2)}) collective-permute-start(bf16[12,1,32,128]{3,0,2,1:T(8,128)(2,1)S(1)} %get-tuple-element.272), channel_id=1, source_target_pairs={{0,1},{1,2},{2,3},{3,4},{4,5},{5,6},{6,7},{7,8},{8,9},{9,10},{10,1... | collective-permute-start | bytes 294920 | tf_op jit(solution)/shard_map/ppermute | solution.py:19
  3.7 1.3 collective-permute-start.1
  5.1 0.9 copy.27
  5.9 0.9 convert_reduce_fusion
  6.9 2.4 %collective-permute-done.1 = bf16[12,1,32,128]{3,0,2,1:T(8,128)(2,1)} collective-permute-done((bf16[12,1,32,128]{3,0,2,1:T(8,128)(2,1)S(1)}, bf16[12,1,32,128]{3,0,2,1:T(8,128)(2,1)}, u32[]{:S(2)}, u32[]{:S(2)}) %collective-permute-start.1) | collective-permute-done | bytes 98336 | tf_op jit(solution)/shard_map/ppermute | solution.py:21
  9.2 2.1 %select_maximum_fusion = bf16[12,6,34,130]{3,0,2,1:T(8,128)(2,1)S(1)} fusion(bf16[12,1,32,128]{3,0,2,1:T(8,128)(2,1)} %collective-permute-done.1, bf16[12,4,32,128]{3,0,2,1:T(8,128)(2,1)} %copy-done.3, bf16[12,1,32,128]{3,0,2,1:T(8,128)(2,1)S(1)} %collective-permute-done), kind=kLoop, calls=%fused_computation.303 | loop fusion | flops 6046560 | bytes 1226304 | tf_op jit(solution)/shard_map/concatenate | solution.py:17
  11.3 26.7 %while.33 = (s32[]{:T(128)}, bf16[4,48,32,128]{3,1,2,0:T(8,128)(2,1)S(1)}, s32[4]{0:T(128)S(1)}, bf16[12,6,34,130]{3,0,2,1:T(8,128)(2,1)S(1)}, bf16[48,324]{0,1:T(8,128)(2,1)S(1)}) while((s32[]{:T(128)}, bf16[4,48,32,128]{3,1,2,0:T(8,128)(2,1)S(1)}, s32[4]{0:T(128)S(1)}, bf16[12,6,34,130]{3,0,2,1:T(8,128)(2,1)S(1)}, ...), condition=%wide.region_2.3_spmd.clone, body=%wide.region_1.2_spmd.sunk.clone | while | flops 136937472 | bytes 22945500 | solution.py:60
  11.3 0.7 dynamic_slice.26
  15.4 0.6 fusion.573
  18.0 0.7 dynamic_slice.26
  22.1 0.6 fusion.573
  24.7 0.7 dynamic_slice.26
  28.8 0.6 fusion.573
  31.4 0.7 dynamic_slice.26
  35.4 0.6 fusion.573
  38.3 3.1 %copy.28 = bf16[48,4,32,128]{0,3,2,1:T(8,128)(2,1)} copy(bf16[48,4,32,128]{3,0,2,1:T(8,128)(2,1)S(1)} %fusion.278) | data formatting | bytes 3145728 | tf_op jit(solution)/shard_map/convert_element_type | solution.py:86
  41.5 8.4 %reduce_max.9 = bf16[48,2,16,64]{0,3,2,1:T(8,128)(2,1)S(1)} reduce(bf16[48,2,2,16,2,64,2]{0,6,5,4,3,2,1:T(2,128)(2,1)} %bitcast.293, bf16[]{:T(256)} %constant.41.clone.1), dimensions={2,4,6}, to_apply=%region_3.4 | reduce | flops 688128 | bytes 1769474 | tf_op jit(solution)/shard_map/reduce_max | solution.py:70
  49.9 5.4 %collective-permute-start.2 = (bf16[48,1,16,64]{0,3,2,1:T(8,128)(2,1)S(1)}, bf16[48,1,16,64]{0,3,2,1:T(8,128)(2,1)S(1)}, u32[]{:S(2)}, u32[]{:S(2)}) collective-permute-start(bf16[48,1,16,64]{0,3,2,1:T(8,128)(2,1)S(1)} %get-tuple-element.270), channel_id=1, source_target_pairs={{0,1},{1,2},{2,3},{3,4},{4,5},{5,6},{6,7},{7,8},{8,9},{9,10},{10,1... | collective-permute-start | bytes 294920 | tf_op jit(solution)/shard_map/ppermute | solution.py:19
  55.3 1.5 collective-permute-start.3
  57.1 1.7 collective-permute-done.3
  59.2 17.8 %while.34 = (s32[]{:T(128)}, bf16[2,96,16,64]{1,3,2,0:T(8,128)(2,1)S(1)}, s32[2]{0:T(128)S(1)}, bf16[48,4,18,66]{0,3,2,1:T(8,128)(2,1)S(1)}, bf16[96,1296]{0,1:T(8,128)(2,1)S(1)}) while((s32[]{:T(128)}, bf16[2,96,16,64]{1,3,2,0:T(8,128)(2,1)S(1)}, s32[2]{0:T(128)S(1)}, bf16[48,4,18,66]{0,3,2,1:T(8,128)(2,1)S(1)}, ...), condition=%wide.region_5.6_spmd.clone, body=%wide.region_4.5_spmd.sunk.clone | while | flops 263553024 | bytes 21135772 | solution.py:60
  59.2 0.7 dynamic_slice.27
  64.1 0.9 fusion.598
  65.5 0.5 convolution_add_fusion.34
  66.0 0.5 fusion.600
  67.5 0.6 fusion.602
  68.2 0.7 dynamic_slice.27
  73.0 0.9 fusion.598
  74.4 0.5 convolution_add_fusion.34
  74.9 0.5 fusion.600
  76.4 0.6 fusion.602
  77.1 0.6 convolution_bitcast_fusion
  78.1 7.5 %broadcast_in_dim.46 = f32[48,2,2,16,2,64,2]{0,6,5,4,3,2,1:T(2,128)} broadcast(f32[48,2,16,64]{0,3,2,1:T(8,128)S(1)} %copy.30), dimensions={0,1,3,5} | broadcast | bytes 3538944 | tf_op jit(solution)/shard_map/broadcast_in_dim | solution.py:77
  85.6 5.1 %copy.31 = f32[48,4,32,128]{3,0,2,1:T(8,128)S(1)} copy(f32[48,4,32,128]{0,3,2,1:T(8,128)} %bitcast.292) | data formatting | bytes 6291456 | tf_op jit(solution)/shard_map/reshape | solution.py:80
  90.7 1.9 %add_convert_fusion = bf16[48,4,32,128]{3,0,2,1:T(8,128)(2,1)S(1)} fusion(f32[48,4,32,128]{3,0,2,1:T(8,128)S(1)} %copy.31, bf16[4,48,32,128]{3,1,2,0:T(8,128)(2,1)} %copy-done.2), kind=kLoop, calls=%fused_computation.281 | loop fusion | flops 4718592 | bytes 6291456 | tf_op jit(solution)/shard_map/convert_element_type | solution.py:90
  92.7 0.7 pad_slice_fusion.10
  94.4 7.2 %collective-permute-start.4 = (bf16[12,1,32,128]{3,0,2,1:T(8,128)(2,1)S(1)}, bf16[12,1,32,128]{3,0,2,1:T(8,128)(2,1)S(1)}, u32[]{:S(2)}, u32[]{:S(2)}) collective-permute-start(bf16[12,1,32,128]{3,0,2,1:T(8,128)(2,1)S(1)} %fusion.344), channel_id=1, source_target_pairs={{0,1},{1,2},{2,3},{3,4},{4,5},{5,6},{6,7},{7,8},{8,9},{9,10},{10,1... | collective-permute-start | bytes 294920 | tf_op jit(solution)/shard_map/ppermute | solution.py:19
  101.5 0.7 pad_slice_fusion.2
  103.2 1.4 collective-permute-start.5
  104.6 3.5 %pad.21 = bf16[48,6,34,130]{3,0,2,1:T(8,128)(2,1)} pad(bf16[48,4,32,128]{3,0,2,1:T(8,128)(2,1)S(1)} %add_convert_fusion, bf16[]{:T(256)} %constant.39.clone.1), padding=0_0x1_1x1_1x1_1 | pad | bytes 4118786 | tf_op jit(solution)/shard_map/jit(_pad)/pad | solution.py:49
  108.2 39.1 %while.35 = (s32[]{:T(128)}, f32[4,12,32,128]{3,1,2,0:T(8,128)S(1)}, s32[4]{0:T(128)S(1)}, bf16[48,6,34,130]{3,0,2,1:T(8,128)(2,1)}, bf16[12,1296]{1,0:T(8,128)(2,1)S(1)}) while((s32[]{:T(128)}, f32[4,12,32,128]{3,1,2,0:T(8,128)S(1)}, s32[4]{0:T(128)S(1)}, bf16[48,6,34,130]{3,0,2,1:T(8,128)(2,1)}, ...), condition=%wide.region_7.8_spmd.clone, body=%wide.region_6.7_spmd.sunk.clone | while | flops 159645696 | bytes 38402460 | solution.py:60
  108.2 0.6 dynamic_slice.28
  110.7 1.8 %dynamic-slice_bitcast_fusion.17 = (bf16[48,34,130]{2,0,1:T(8,128)(2,1)S(1)}, bf16[48,34,130]{2,0,1:T(8,128)(2,1)S(1)}, bf16[48,34,130]{2,0,1:T(8,128)(2,1)S(1)}) fusion(bf16[48,6,34,130]{3,0,2,1:T(8,128)(2,1)} %get-tuple-element.744, s32[]{:T(128)S(6)} %add.376, s32[]{:T(128)S(6)} %add.377, s32[]{:T(128)S(6)} %select_n.17), kind=kLoop, calls=%fused_computation.240.clone.1.clone | loop fusion | bytes 2545932 | tf_op jit(solution)/shard_map/while/body/eval_jaxpr/squeeze | solution.py:57
  112.5 0.8 fusion.621
  114.2 1.8 %fusion.625 = (bf16[48,32,128]{2,0,1:T(8,128)(2,1)S(1)}, bf16[48,32,128]{2,0,1:T(8,128)(2,1)S(1)}, bf16[48,32,128]{2,0,1:T(8,128)(2,1)S(1)}, bf16[48,32,128]{2,0...) fusion(bf16[48,34,130]{2,0,1:T(8,128)(2,1)S(1)} %get-tuple-elem, ...), kind=kLoop, calls=%fused_computation.419.clone.1.clone | loop fusion | bytes 14155776 | tf_op jit(solution)/shard_map/while/body/eval_jaxpr/slice | solution.py:36
  118.0 0.6 dynamic_slice.28
  120.5 1.8 %dynamic-slice_bitcast_fusion.17 = (bf16[48,34,130]{2,0,1:T(8,128)(2,1)S(1)}, bf16[48,34,130]{2,0,1:T(8,128)(2,1)S(1)}, bf16[48,34,130]{2,0,1:T(8,128)(2,1)S(1)}) fusion(bf16[48,6,34,130]{3,0,2,1:T(8,128)(2,1)} %get-tuple-element.744, s32[]{:T(128)S(6)} %add.376, s32[]{:T(128)S(6)} %add.377, s32[]{:T(128)S(6)} %select_n.17), kind=kLoop, calls=%fused_computation.240.clone.1.clone | loop fusion | bytes 2545932 | tf_op jit(solution)/shard_map/while/body/eval_jaxpr/squeeze | solution.py:57
  122.3 0.8 fusion.621
  124.0 1.8 %fusion.625 = (bf16[48,32,128]{2,0,1:T(8,128)(2,1)S(1)}, bf16[48,32,128]{2,0,1:T(8,128)(2,1)S(1)}, bf16[48,32,128]{2,0,1:T(8,128)(2,1)S(1)}, bf16[48,32,128]{2,0...) fusion(bf16[48,34,130]{2,0,1:T(8,128)(2,1)S(1)} %get-tuple-elem, ...), kind=kLoop, calls=%fused_computation.419.clone.1.clone | loop fusion | bytes 14155776 | tf_op jit(solution)/shard_map/while/body/eval_jaxpr/slice | solution.py:36
  127.7 0.6 dynamic_slice.28
  130.3 1.8 %dynamic-slice_bitcast_fusion.17 = (bf16[48,34,130]{2,0,1:T(8,128)(2,1)S(1)}, bf16[48,34,130]{2,0,1:T(8,128)(2,1)S(1)}, bf16[48,34,130]{2,0,1:T(8,128)(2,1)S(1)}) fusion(bf16[48,6,34,130]{3,0,2,1:T(8,128)(2,1)} %get-tuple-element.744, s32[]{:T(128)S(6)} %add.376, s32[]{:T(128)S(6)} %add.377, s32[]{:T(128)S(6)} %select_n.17), kind=kLoop, calls=%fused_computation.240.clone.1.clone | loop fusion | bytes 2545932 | tf_op jit(solution)/shard_map/while/body/eval_jaxpr/squeeze | solution.py:57
  132.1 0.8 fusion.621
  133.8 1.8 %fusion.625 = (bf16[48,32,128]{2,0,1:T(8,128)(2,1)S(1)}, bf16[48,32,128]{2,0,1:T(8,128)(2,1)S(1)}, bf16[48,32,128]{2,0,1:T(8,128)(2,1)S(1)}, bf16[48,32,128]{2,0...) fusion(bf16[48,34,130]{2,0,1:T(8,128)(2,1)S(1)} %get-tuple-elem, ...), kind=kLoop, calls=%fused_computation.419.clone.1.clone | loop fusion | bytes 14155776 | tf_op jit(solution)/shard_map/while/body/eval_jaxpr/slice | solution.py:36
  137.5 0.6 dynamic_slice.28
  140.0 1.8 %dynamic-slice_bitcast_fusion.17 = (bf16[48,34,130]{2,0,1:T(8,128)(2,1)S(1)}, bf16[48,34,130]{2,0,1:T(8,128)(2,1)S(1)}, bf16[48,34,130]{2,0,1:T(8,128)(2,1)S(1)}) fusion(bf16[48,6,34,130]{3,0,2,1:T(8,128)(2,1)} %get-tuple-element.744, s32[]{:T(128)S(6)} %add.376, s32[]{:T(128)S(6)} %add.377, s32[]{:T(128)S(6)} %select_n.17), kind=kLoop, calls=%fused_computation.240.clone.1.clone | loop fusion | bytes 2545932 | tf_op jit(solution)/shard_map/while/body/eval_jaxpr/squeeze | solution.py:57
  141.9 0.8 fusion.621
  143.6 1.8 %fusion.625 = (bf16[48,32,128]{2,0,1:T(8,128)(2,1)S(1)}, bf16[48,32,128]{2,0,1:T(8,128)(2,1)S(1)}, bf16[48,32,128]{2,0,1:T(8,128)(2,1)S(1)}, bf16[48,32,128]{2,0...) fusion(bf16[48,34,130]{2,0,1:T(8,128)(2,1)S(1)} %get-tuple-elem, ...), kind=kLoop, calls=%fused_computation.419.clone.1.clone | loop fusion | bytes 14155776 | tf_op jit(solution)/shard_map/while/body/eval_jaxpr/slice | solution.py:36
  147.5 0.5 copy-done.8
  148.0 0.7 fusion.340
  148.8 0.5 reshape.28
  149.4 1.2 reshape.29
  151.1 14.8 %all_to_all.5 = bf16[16,2,1536]{2,1,0:T(2,128)(2,1)S(1)} all-to-all(bf16[16,2,1536]{2,1,0:T(2,128)(2,1)S(1)} %reshape.30), channel_id=1, replica_groups=mesh['grp'=2,'gz'=16] {'gz'}, dimensions={0} | all-to-all | bytes 196608 | tf_op jit(solution)/shard_map/all_to_all | solution.py:143
  166.0 0.6 copy.60
  (145 shorter events, 35.6 us)
Async XLA Ops:
  0.0 77.1 %copy-start = (bf16[48,96]{1,0:T(8,128)(2,1)S(1)}, bf16[48,96]{1,0:T(8,128)(2,1)}, u32[]{:S(2)}) copy-start(bf16[48,96]{1,0:T(8,128)(2,1)} %param.17) | copy-start | bytes 27652
  1.3 2.5 %copy-start.3 = (bf16[12,4,32,128]{3,0,2,1:T(8,128)(2,1)}, bf16[12,4,32,128]{3,0,2,1:T(8,128)(2,1)S(1)}, u32[]{:S(2)}) copy-start(bf16[12,4,32,128]{3,0,2,1:T(8,128)(2,1)S(1)} %copy.24) | copy-start | bytes 1179652
  1.3 5.5 %collective-permute-start = (bf16[12,1,32,128]{3,0,2,1:T(8,128)(2,1)S(1)}, bf16[12,1,32,128]{3,0,2,1:T(8,128)(2,1)S(1)}, u32[]{:S(2)}, u32[]{:S(2)}) collective-permute-start(bf16[12,1,32,128]{3,0,2,1:T(8,128)(2,1)S(1)} %get-tuple-element.272), channel_id=1, source_target_pairs={{0,1},{1,2},{2,3},{3,4},{4,5},{5,6},{6,7},{7,8},{8,9},{9,10},{10,1... | collective-permute-start | bytes 294920 | tf_op jit(solution)/shard_map/ppermute | solution.py:19
  3.7 5.5 %collective-permute-start.1 = (bf16[12,1,32,128]{3,0,2,1:T(8,128)(2,1)S(1)}, bf16[12,1,32,128]{3,0,2,1:T(8,128)(2,1)}, u32[]{:S(2)}, u32[]{:S(2)}) collective-permute-start(bf16[12,1,32,128]{3,0,2,1:T(8,128)(2,1)S(1)} %get-tuple-element.273), channel_id=1, source_target_pairs={{1,0},{2,1},{3,2},{4,3},{5,4},{6,5},{7,6},{8,7},{9,8},{10,9},{11,1... | collective-permute-start | bytes 294920 | tf_op jit(solution)/shard_map/ppermute | solution.py:21
  38.0 3.5 %copy-start.2 = (bf16[4,48,32,128]{3,1,2,0:T(8,128)(2,1)}, bf16[4,48,32,128]{3,1,2,0:T(8,128)(2,1)S(1)}, u32[]{:S(2)}) copy-start(bf16[4,48,32,128]{3,1,2,0:T(8,128)(2,1)S(1)} %get-tuple-element.86) | copy-start | bytes 4718596
  41.5 15.3 %copy-start.9 = (s32[1,32]{1,0:T(1,128)S(1)}, s32[1,32]{1,0:T(1,128)}, u32[]{:S(2)}) copy-start(s32[1,32]{1,0:T(1,128)} %param.21) | copy-start | bytes 388
  41.5 15.4 %copy-start.5 = (bf16[96,1296]{1,0:T(8,128)(2,1)S(1)}, bf16[96,1296]{1,0:T(8,128)(2,1)}, u32[]{:S(2)}) copy-start(bf16[96,1296]{1,0:T(8,128)(2,1)} %param.16) | copy-start | bytes 746500
  49.9 7.2 %collective-permute-start.2 = (bf16[48,1,16,64]{0,3,2,1:T(8,128)(2,1)S(1)}, bf16[48,1,16,64]{0,3,2,1:T(8,128)(2,1)S(1)}, u32[]{:S(2)}, u32[]{:S(2)}) collective-permute-start(bf16[48,1,16,64]{0,3,2,1:T(8,128)(2,1)S(1)} %get-tuple-element.270), channel_id=1, source_target_pairs={{0,1},{1,2},{2,3},{3,4},{4,5},{5,6},{6,7},{7,8},{8,9},{9,10},{10,1... | collective-permute-start | bytes 294920 | tf_op jit(solution)/shard_map/ppermute | solution.py:19
  55.3 3.4 %collective-permute-start.3 = (bf16[48,1,16,64]{0,3,2,1:T(8,128)(2,1)S(1)}, bf16[48,1,16,64]{0,3,2,1:T(8,128)(2,1)S(1)}, u32[]{:S(2)}, u32[]{:S(2)}) collective-permute-start(bf16[48,1,16,64]{0,3,2,1:T(8,128)(2,1)S(1)} %get-tuple-element.271), channel_id=1, source_target_pairs={{1,0},{2,1},{3,2},{4,3},{5,4},{6,5},{7,6},{8,7},{9,8},{10,9},{11,1... | collective-permute-start | bytes 294920 | tf_op jit(solution)/shard_map/ppermute | solution.py:21
  92.6 0.8 copy-start.7
  94.4 53.0 %collective-permute-start.4 = (bf16[12,1,32,128]{3,0,2,1:T(8,128)(2,1)S(1)}, bf16[12,1,32,128]{3,0,2,1:T(8,128)(2,1)S(1)}, u32[]{:S(2)}, u32[]{:S(2)}) collective-permute-start(bf16[12,1,32,128]{3,0,2,1:T(8,128)(2,1)S(1)} %fusion.344), channel_id=1, source_target_pairs={{0,1},{1,2},{2,3},{3,4},{4,5},{5,6},{6,7},{7,8},{8,9},{9,10},{10,1... | collective-permute-start | bytes 294920 | tf_op jit(solution)/shard_map/ppermute | solution.py:19
  103.2 5.0 %copy-start.4 = (f32[4,12,32,128]{3,1,2,0:T(8,128)S(1)}, f32[4,12,32,128]{3,1,2,0:T(8,128)}, u32[]{:S(2)}) copy-start(f32[4,12,32,128]{3,1,2,0:T(8,128)} %custom-call) | copy-start | bytes 2359300
  103.2 44.2 %collective-permute-start.5 = (bf16[12,1,32,128]{3,0,2,1:T(8,128)(2,1)S(1)}, bf16[12,1,32,128]{3,0,2,1:T(8,128)(2,1)S(1)}, u32[]{:S(2)}, u32[]{:S(2)}) collective-permute-start(bf16[12,1,32,128]{3,0,2,1:T(8,128)(2,1)S(1)} %fusion.341), channel_id=1, source_target_pairs={{1,0},{2,1},{3,2},{4,3},{5,4},{6,5},{7,6},{8,7},{9,8},{10,9},{11,1... | collective-permute-start | bytes 294920 | tf_op jit(solution)/shard_map/ppermute | solution.py:21
  147.3 0.7 copy-start.8
  148.7 1.9 %copy-start.6 = (s32[1,32]{1,0:T(1,128)S(1)}, s32[1,32]{1,0:T(1,128)}, u32[]{:S(2)}) copy-start(s32[1,32]{1,0:T(1,128)} %param.20) | copy-start | bytes 388
  148.8 17.8 %copy-start.1 = (bf16[48,96]{1,0:T(8,128)(2,1)S(1)}, bf16[48,96]{1,0:T(8,128)(2,1)}, u32[]{:S(2)}) copy-start(bf16[48,96]{1,0:T(8,128)(2,1)} %param.17) | copy-start | bytes 27652
where the time goes:
time: 168 us; the launch traced here: 167 us
  local copies, waits for them, and re-layouts  57.6 us (34%)
  matrix products  35.7 us (21%)
  loops' own time  20.7 us (12%)
  starting transfers between devices  19.2 us (11%)
  blocking collectives  14.8 us (9%)
  other arithmetic  14.1 us (8%)
  waiting for transfers between devices  4.05 us (2%)
    dot_general x96, matrix products, plane_terms(): jnp.einsum('oi,iyx->oyx', weight_part, stacked, preferred_element_type=jn...  34 us
    another operation x3, loops' own time, convolve(): planes = lax.map(one_plane, jnp.arange(out_depth, dtype=jnp.int32))  20.7 us
    slice x22, local copies, waits for them, and re-layouts, plane_terms(): padded_plane[:, offset_y:offset_y + rows, offset_x:offset_x + columns]  18.1 us
    ppermute x3, starting transfers between devices, padded_2(): lax.ppermute(tail, axis, [(i, (i + 1) % count) for i in range(ends)])  15 us
    all_to_all x1, blocking collectives, on_device(): lax.all_to_all(outgoing, 'gz', split_axis=0, concat_axis=0, tiled=True)  14.8 us
    reduce_max x1, other arithmetic, maxpool(): volume.reshape(shape[0], shape[1] // 2, 2, shape[2] // 2, 2, shape[3] //...  8.37 us
    squeeze x10, local copies, waits for them, and re-layouts, one_plane(): window_planes[:, 2]  7.71 us
    broadcast_in_dim x1, local copies, waits for them, and re-layouts, upsample(): jnp.broadcast_to(volume[:, :, None, :, None, :, None], (shape[0], shape[1...  7.5 us
  transfers between devices with their start and end apart: 6, of which 2 were waited for; matrix products, arithmetic and copies ran while one was open for 23% of the time, Pallas kernels for 0%

commit v1 on v0

v1 whole, which is shorter than its diff:
```python
import functools

import jax
import jax.numpy as jnp
from jax import lax
from jax.experimental import pallas as pl
from jax.experimental.pallas import tpu as pltpu
from jax.sharding import PartitionSpec as P

BY = 8
BX = 16
SEND_CAP = 2
HALO = 3
F32 = jnp.float32
BF16 = jnp.bfloat16


def iota(shape, dim):
    return lax.broadcasted_iota(jnp.int32, shape, dim)


def beside(value, width):
    lane = iota(value.shape, 1) % width
    left = jnp.where(lane == 0, jnp.zeros_like(value), pltpu.roll(value, 1, 1))
    right = jnp.where(
        lane == width - 1, jnp.zeros_like(value), pltpu.roll(value, value.shape[1] - 1, 1)
    )
    return left, value, right


def trunk_kernel(
    flags,
    features,
    from_pair,
    from_next,
    w_first,
    w_second,
    w_lift,
    w_merge,
    inner,
    to_pair,
    to_next,
    plain,
    cols_1,
    first,
    cols_2,
    cols_3,
    total,
    edge,
):
    c0, depth, rows, lanes = features.shape
    c1 = w_lift.shape[0]
    c2 = w_lift.shape[1]
    half_rows = rows // 2
    wide = depth + 2 * HALO
    odd = flags[0]
    low_ok = flags[1]
    high_ok = flags[2]

    for z in range(HALO):
        for c in range(c0):
            a = from_pair[c, z].astype(F32)
            b = from_next[c, z].astype(F32)
            plain[z, c] = jnp.where(odd == 1, a, b)
            plain[HALO + depth + z, c] = jnp.where(odd == 1, b, a)
    for z in range(depth):
        for c in range(c0):
            plain[HALO + z, c] = features[c, z].astype(F32)

    pad_1 = jnp.zeros((cols_1.shape[2], lanes), BF16)
    for z in range(wide):
        cols_1[z, 0] = pad_1
        cols_1[z, rows + 1] = pad_1

    gap = jnp.zeros((16 - c0, lanes), F32)

    def spread_1(z, carry):
        flat = plain.at[z].reshape(c0 * rows, lanes)
        for y in range(rows):
            face = flat[pl.ds(y, c0, stride=rows), :]
            face = jnp.concatenate([face, gap], axis=0)
            cols_1[z, y + 1] = jnp.concatenate(beside(face, lanes), axis=0).astype(BF16)
        return carry

    lax.fori_loop(0, wide, spread_1, 0)

    weight_1 = w_first[...]
    run_1 = 16

    def conv_1(i, carry):
        z = i // (rows // run_1)
        y = (i % (rows // run_1)) * run_1
        x = jnp.concatenate(
            [
                jnp.concatenate(
                    [cols_1[z + a, y + b + j] for a in range(3) for b in range(3)], axis=0
                )
                for j in range(run_1)
            ],
            axis=1,
        )
        out = jnp.dot(weight_1, x, preferred_element_type=F32)
        out = jnp.maximum(out, 0.0).astype(BF16)
        for j in range(run_1):
            first[z, y + j] = out[:, j * lanes : (j + 1) * lanes]
        return carry

    lax.fori_loop(0, (wide - 2) * (rows // run_1), conv_1, 0)

    pick = (iota((2 * lanes, lanes), 0) == 2 * iota((2 * lanes, lanes), 1)).astype(BF16)
    lane = iota((c1, lanes), 1)
    low_half = lane < lanes // 2
    keep_low = jnp.logical_or(jnp.logical_not(low_half), low_ok == 1)
    keep_high = jnp.logical_or(low_half, high_ok == 1)
    pad_2 = jnp.zeros((3 * c1, lanes), BF16)
    for a in range(3):
        cols_2[a, 0] = pad_2
        cols_2[a, half_rows + 1] = pad_2

    def pool(y, carry):
        tops = []
        for p in range(4):
            m = jnp.maximum(
                jnp.maximum(first[2 * p, 2 * y], first[2 * p, 2 * y + 1]),
                jnp.maximum(first[2 * p + 1, 2 * y], first[2 * p + 1, 2 * y + 1]),
            ).astype(F32)
            tops.append(jnp.maximum(m, pltpu.roll(m, lanes - 1, 1)).astype(BF16))
        both = jnp.concatenate(
            [
                jnp.concatenate([tops[0], tops[1]], axis=1),
                jnp.concatenate([tops[2], tops[3]], axis=1),
            ],
            axis=0,
        )
        packed = jnp.dot(both, pick, preferred_element_type=F32)
        low = jnp.where(keep_low, packed[:c1], 0.0)
        high = jnp.where(keep_high, packed[c1:], 0.0)
        middle = pltpu.roll(jnp.where(low_half, high, low), lanes // 2, 1)
        for a, value in enumerate((low, middle, high)):
            cols_2[a, y + 1] = jnp.concatenate(beside(value, lanes // 2), axis=0).astype(BF16)
        return carry

    lax.fori_loop(0, half_rows, pool, 0)

    weight_2 = w_second[...]
    weight_l = w_lift[...]
    widen = (iota((lanes, 2 * lanes), 0) == iota((lanes, 2 * lanes), 1) // 2).astype(BF16)
    run_2 = 4

    def conv_2(i, carry):
        y = i * run_2
        x = jnp.concatenate(
            [
                jnp.concatenate(
                    [cols_2[a, y + b + j] for a in range(3) for b in range(3)], axis=0
                )
                for j in range(run_2)
            ],
            axis=1,
        )
        second = jnp.dot(weight_2, x, preferred_element_type=F32)
        second = jnp.maximum(second, 0.0).astype(BF16)
        stacked = jnp.concatenate(
            [second[:, j * lanes : (j + 1) * lanes] for j in range(run_2)], axis=0
        )
        stacked = jnp.dot(stacked, widen, preferred_element_type=F32).astype(BF16)
        spread = jnp.concatenate(
            [stacked[j * c2 : (j + 1) * c2] for j in range(run_2)], axis=1
        )
        lifted = jnp.dot(weight_l, spread, preferred_element_type=F32)
        for j in range(run_2):
            for zz in range(2):
                at = (2 * j + zz) * lanes
                value = lifted[:, at : at + lanes]
                for dz in range(2):
                    for dy in range(2):
                        z = 2 * zz + dz
                        row = 2 * (y + j) + dy
                        merged = value + first[z + 2, row].astype(F32)
                        merged = merged.astype(BF16).astype(F32)
                        cols_3[z, row] = jnp.concatenate(beside(merged, lanes), axis=0).astype(
                            BF16
                        )
        return carry

    lax.fori_loop(0, half_rows // run_2, conv_2, 0)

    total[...] = jnp.zeros_like(total)
    weight_3 = w_merge[...]
    run_3 = 8

    def conv_3(i, carry):
        z = i // (rows // run_3)
        y = (i % (rows // run_3)) * run_3
        x = jnp.concatenate([cols_3[z, y + j] for j in range(run_3)], axis=1)
        out = jnp.dot(weight_3, x, preferred_element_type=F32)
        for a in range(3):
            for k in range(run_3 + 2):
                term = None
                for b in range(3):
                    j = k - 2 + b
                    if 0 <= j < run_3:
                        at = (a * 3 + b) * 16
                        value = out[at : at + 16, j * lanes : (j + 1) * lanes]
                        term = value if term is None else term + value
                total[z + 2 - a, y + k] += term
        return carry

    lax.fori_loop(0, depth * (rows // run_3), conv_3, 0)

    cu = edge.shape[0] // rows
    for target, plane in ((to_pair, jnp.where(odd == 1, 0, depth + 1)),
                          (to_next, jnp.where(odd == 1, depth + 1, 0))):
        for y in range(rows):
            edge[y * cu : (y + 1) * cu] = total[plane, y + 1, 0:cu]
        target[...] = edge[...].astype(BF16)
    for z in range(depth):
        inner[z] = total[z + 1, 1 : rows + 1]


def tail_kernel(flags, inner, from_pair, from_next, w_head, tissue, owners, out, edge, shown):
    depth, rows, _, lanes = inner.shape
    cu = from_pair.shape[0] // rows
    odd = flags[0]
    a = from_pair[...].astype(F32)
    b = from_next[...].astype(F32)
    edge[0] = jnp.where(odd == 1, a, b)
    edge[1] = jnp.where(odd == 1, b, a)
    head = w_head[...]
    gap = jnp.zeros((16 - cu, lanes), F32)
    run = 8
    for y0 in range(0, rows, run):
        columns = []
        for y in range(y0, y0 + run):
            parts = []
            for z in range(depth):
                value = inner[z, y]
                if z == 0:
                    value = value + jnp.concatenate([edge[0, y * cu : (y + 1) * cu], gap], axis=0)
                if z == depth - 1:
                    value = value + jnp.concatenate([edge[1, y * cu : (y + 1) * cu], gap], axis=0)
                value = jnp.maximum(value, 0.0)
                for _ in range(3):
                    part = value.astype(BF16)
                    parts.append(part)
                    value = value - part.astype(F32)
            columns.append(jnp.concatenate(parts, axis=0))
        logits = jnp.dot(head, jnp.concatenate(columns, axis=1), preferred_element_type=F32)
        chance = jax.nn.sigmoid(logits)
        for j in range(run):
            shown[(y0 + j) * 16 : (y0 + j + 1) * 16] = chance[:, j * lanes : (j + 1) * lanes]

    sub = iota((BY, lanes), 0)
    group = iota((BY, lanes), 1) // BX
    faces = 3 * depth
    tiles = []
    for f in range(faces):
        blocks = []
        for by in range(rows // BY):
            v = shown[pl.ds(by * BY * 16 + f, BY, stride=16), :]
            for k in (1, 2, 4):
                s_bit = (sub // k) % 2
                g_bit = (group // k) % 2
                down = pltpu.roll(pltpu.roll(v, BY - k, 0), k * BX, 1)
                up = pltpu.roll(pltpu.roll(v, k, 0), lanes - k * BX, 1)
                v = jnp.where(s_bit == g_bit, v, jnp.where(s_bit < g_bit, down, up))
            blocks.append(v)
        tiles.append(jnp.concatenate(blocks, axis=0))
    tiles = jnp.concatenate(tiles, axis=1).astype(BF16)

    count = tissue.shape[1]
    slots = out.shape[0]
    own = jnp.broadcast_to(owners[...], (count, count))
    seen = jnp.broadcast_to(tissue[...], (count, count))
    r = iota((count, count), 0)
    c = iota((count, count), 1)
    own_column = jnp.sum(jnp.where(r == c, own, 0), axis=1, keepdims=True)
    seen_column = jnp.sum(jnp.where(r == c, seen, 0), axis=1, keepdims=True)
    before = jnp.where(jnp.logical_and(own_column == own, r < c), 1, 0)
    slot = owners[...] * SEND_CAP + jnp.sum(before, axis=0, keepdims=True)
    slot_pick = (iota((slots, count), 0) == slot).astype(F32).astype(BF16)
    blocks = tiles.shape[0]
    block_pick = (seen_column == iota((count, blocks), 1)).astype(F32).astype(BF16)
    select = jnp.dot(slot_pick, block_pick, preferred_element_type=F32).astype(BF16)
    out[...] = jnp.dot(select, tiles, preferred_element_type=F32).astype(BF16)


def on_device(features, w_first, w_second, w_lift, w_merge, w_affine, tissue, owners):
    c0, depth, rows, lanes = features.shape
    c1, c2 = w_lift.shape
    cu = w_merge.shape[0]
    devices = lax.axis_size("gz")
    here = lax.axis_index("gz")
    odd = here % 2
    flags = jnp.stack([odd, (here > 0).astype(jnp.int32), (here < devices - 1).astype(jnp.int32)])
    pair = [(i, i ^ 1) for i in range(devices)]
    after = [(i, i + 1) for i in range(1, devices - 1, 2)]
    after = after + [(j, i) for i, j in after]

    lower = lax.slice_in_dim(features, 0, HALO, axis=1)
    upper = lax.slice_in_dim(features, depth - HALO, depth, axis=1)
    from_next = lax.ppermute(jnp.where(odd == 1, upper, lower), "gz", after)
    from_pair = lax.ppermute(jnp.where(odd == 1, lower, upper), "gz", pair)

    first_cols = jnp.pad(w_first.reshape(c1, 27, c0), ((0, 0), (0, 0), (0, 16 - c0)))
    first_cols = first_cols.reshape(c1, 27 * 16)
    merge_rows = w_merge.reshape(cu, 9, 3 * c1).transpose(1, 0, 2)
    merge_rows = jnp.pad(merge_rows, ((0, 0), (0, 16 - cu), (0, 0))).reshape(9 * 16, 3 * c1)
    head = jnp.pad(w_affine, ((0, 0), (0, 16 - cu)))
    head = jnp.tile(head, (1, 3))
    head = jnp.einsum("ac,zw->azwc", head, jnp.eye(depth, dtype=head.dtype))
    head = jnp.pad(head.reshape(3 * depth, -1), ((0, 16 - 3 * depth), (0, 0)))

    vmem = pl.BlockSpec(memory_space=pltpu.VMEM)
    smem = pl.BlockSpec(memory_space=pltpu.SMEM)
    shape = jax.ShapeDtypeStruct
    wide = depth + 2 * HALO
    inner, to_pair, to_next = pl.pallas_call(
        trunk_kernel,
        out_shape=(
            shape((depth, rows, 16, lanes), F32),
            shape((rows * cu, lanes), BF16),
            shape((rows * cu, lanes), BF16),
        ),
        in_specs=[smem] + [vmem] * 7,
        out_specs=(vmem,) * 3,
        scratch_shapes=[
            pltpu.VMEM((wide, c0, rows, lanes), F32),
            pltpu.VMEM((wide, rows + 2, 48, lanes), BF16),
            pltpu.VMEM((wide - 2, rows, c1, lanes), BF16),
            pltpu.VMEM((3, rows // 2 + 2, 3 * c1, lanes), BF16),
            pltpu.VMEM((depth, rows, 3 * c1, lanes), BF16),
            pltpu.VMEM((depth + 2, rows + 2, 16, lanes), F32),
            pltpu.VMEM((rows * cu, lanes), F32),
        ],
        name="trunk",
    )(flags, features, from_pair, from_next, first_cols, w_second, w_lift, merge_rows)

    edge_next = lax.ppermute(to_next, "gz", after)
    edge_pair = lax.ppermute(to_pair, "gz", pair)
    outgoing = pl.pallas_call(
        tail_kernel,
        out_shape=shape((devices * SEND_CAP, 3 * depth * BY * BX), BF16),
        in_specs=[smem] + [vmem] * 6,
        out_specs=vmem,
        scratch_shapes=[
            pltpu.VMEM((2, rows * cu, lanes), F32),
            pltpu.VMEM((rows * 16, lanes), F32),
        ],
        name="tail",
    )(flags, inner, edge_pair, edge_next, head, tissue, owners)
    outgoing = outgoing.reshape(devices, SEND_CAP, -1)
    return lax.all_to_all(outgoing, "gz", split_axis=0, concat_axis=0, tiled=True)[None]


def solution(mesh):
    placed = (
        P(None, ("grp", "gz"), None, None),
        P(),
        P(),
        P(),
        P(),
        P(),
        P(("grp", "gz"), None),
        P(("grp", "gz"), None),
    )
    return jax.shard_map(
        on_device,
        mesh=mesh,
        in_specs=placed,
        out_specs=P(("grp", "gz"), None, None, None),
        check_vma=False,
    )
```

time: 168 us -> 64 us (0.38)
  local copies, waits for them, and re-layouts: 57.6 us -> 5.7 us
  matrix products: 35.7 us -> 0 us
  Pallas kernels: 0 us -> 27.1 us
  loops' own time: 20.7 us -> 0 us
  other arithmetic: 14.1 us -> 1.77 us
  starting transfers between devices: 19.2 us -> 9.82 us
  blocking collectives: 14.8 us -> 19.1 us
  waiting for transfers between devices: 4.05 us -> 0.01 us
    dot_general x99 -> x0, matrix products: 35.7 us -> none  [the longest x96 34 us: plane_terms(): jnp.einsum('oi,iyx->oyx', weight_part, stacked, preferred_element_type=jn...]
    pallas_call x0 -> x2, Pallas kernels: none -> 27.1 us  [the longest x1 24.3 us: on_device(): pl.pallas_call(trunk_kernel, out_shape=(shape((depth, rows, 16, lanes), F...]
    another operation x3 -> x0, loops' own time: 20.7 us -> none  [convolve(): planes = lax.map(one_plane, jnp.arange(out_depth, dtype=jnp.int32))]
    slice x25 -> x0, local copies, waits for them, and re-layouts: 18.2 us -> none  [the longest x22 18.1 us: plane_terms(): padded_plane[:, offset_y:offset_y + rows, offset_x:offset_x + columns]]
    ppermute x6 -> x4, starting transfers between devices: 19.2 us -> 9.82 us  [the longest x1 7.94 us: on_device(): edge_pair = lax.ppermute(to_pair, 'gz', pair)]
    reduce_max x1 -> x0, other arithmetic: 8.37 us -> none  [maxpool(): volume.reshape(shape[0], shape[1] // 2, 2, shape[2] // 2, 2, shape[3] //...]
    squeeze x11 -> x0, local copies, waits for them, and re-layouts: 7.76 us -> none  [the longest x10 7.71 us: one_plane(): window_planes[:, 2]]
    broadcast_in_dim x1 -> x0, local copies, waits for them, and re-layouts: 7.5 us -> none  [upsample(): jnp.broadcast_to(volume[:, :, None, :, None, :, None], (shape[0], shape[1...]
  transfers between devices with their start and end apart: 6 -> 4, of which waited for: 2 -> 0; matrix products, arithmetic and copies ran while one was open for 23% -> 5% of each run, Pallas kernels for 0% -> 0%
where the time goes in v1:
time: 64 us; the launch traced here: 63.7 us
  Pallas kernels  27.1 us (42%)
  blocking collectives  19.1 us (30%)
  starting transfers between devices  9.82 us (15%)
  local copies, waits for them, and re-layouts  5.7 us (9%)
  other arithmetic  1.77 us (3%)
    pallas_call x1, Pallas kernels, on_device(): pl.pallas_call(trunk_kernel, out_shape=(shape((depth, rows, 16, lanes), F...  24.3 us
    all_to_all x1, blocking collectives, on_device(): lax.all_to_all(outgoing, 'gz', split_axis=0, concat_axis=0, tiled=True)  19.1 us
    ppermute x1, starting transfers between devices, on_device(): edge_pair = lax.ppermute(to_pair, 'gz', pair)  7.94 us
    pallas_call x1, Pallas kernels, on_device(): pl.pallas_call(tail_kernel, out_shape=shape((devices * SEND_CAP, 3 * dept...  2.85 us
    unnamed x17, local copies, waits for them, and re-layouts  2.36 us
  transfers between devices with their start and end apart: 4, of which 0 were waited for; matrix products, arithmetic and copies ran while one was open for 5% of the time, Pallas kernels for 0%

profile of v1, /device:TPU:0, one launch (start us, length us, event | category | flops | bytes accessed | tf_op | source)
XLA Modules:
  0.0 63.7 jit_solution(9769906515653165894)
XLA Ops:
  0.0 0.0 copy-start.5
  0.0 1.1 %broadcast_select_fusion = (bf16[12,3,32,128]{3,2,1,0:T(8,128)(2,1)S(1)}, bf16[12,3,32,128]{3,2,1,0:T(8,128)(2,1)S(1)}) fusion(pred[]{:T(512)S(6)} %eq.9, bf16[12,4,32,128]{3,2,1,0:T(8,128)(2,1)} %features.1), kind=kLoop, calls=%fused_computation | loop fusion | flops 294912 | bytes 1179649 | tf_op jit(solution)/shard_map/jit(_where)/select_n | solution.py:302
  1.1 0.6 collective-permute-start
  1.7 0.7 %collective-permute-start.1 = (bf16[12,3,32,128]{3,2,1,0:T(8,128)(2,1)S(1)}, bf16[12,3,32,128]{3,2,1,0:T(8,128)(2,1)S(1)}, u32[]{:S(2)}, u32[]{:S(2)}) collective-permute-start(bf16[12,3,32,128]{3,2,1,0:T(8,128)(2,1)S(1)} %get-tuple-element.11), channel_id=1, source_target_pairs={{1,2},{3,4},{5,6},{7,8},{9,10},{11,12},{13,14},{2,1},{4,3},{6,5},{... | collective-permute-start | bytes 884744 | tf_op jit(solution)/shard_map/ppermute | solution.py:302
  2.3 0.0 copy-done.5
  2.4 0.1 copy.10
  2.6 0.0 copy-start.4
  2.6 0.7 %copy.12.w_first = bf16[48,432]{1,0:T(8,128)(2,1)} copy(bf16[48,432]{0,1:T(8,128)(2,1)S(1)} %bitcast.11) | data formatting | bytes 82944 | tf_op jit(solution)/shard_map/reshape | solution.py:306
  3.3 0.1 copy-done.4
  3.4 0.2 reshape.24
  3.6 0.0 copy-start.6
  3.6 0.6 %pad.17.clone = bf16[9,16,144]{2,1,0:T(8,128)(2,1)} pad(bf16[9,12,144]{2,1,0:T(8,128)(2,1)S(1)} %copy.13, bf16[]{:T(256)} %constant.22.clone.1), padding=0_0x0_4x0_0 | pad | bytes 72578 | tf_op jit(solution)/shard_map/jit(_pad)/pad | solution.py:308
  4.2 0.0 copy-done.6
  4.3 0.1 tile.10
  4.4 0.6 pad_add_fusion.flags
  4.9 0.0 collective-permute-done.from_pair
  4.9 0.0 copy-start
  5.0 0.0 collective-permute-done.1.from_next
  5.0 0.0 copy-start.1
  5.0 0.7 %copy-done = bf16[12,3,32,128]{3,2,1,0:T(8,128)(2,1)} copy-done((bf16[12,3,32,128]{3,2,1,0:T(8,128)(2,1)}, bf16[12,3,32,128]{3,2,1,0:T(8,128)(2,1)S(1)}, u32[]{:S(2)}) %copy-start) | copy-done | bytes 294936
  5.7 0.1 copy-done.1
  5.8 24.3 %trunk.1 = (f32[4,32,16,128]{3,2,1,0:T(8,128)}, bf16[384,128]{1,0:T(8,128)(2,1)}, bf16[384,128]{1,0:T(8,128)(2,1)}) custom-call(s32[3]{0:T(128)} %pad_add_fusion.flags, bf16[12,4,32,128]{3,2,1,0:T(8,128)(2,1)} %features.1, bf16[12,3,32,128]{3,2,1,0:T(8,128)(2,1)} %copy-done, bf16[12,3,32,128]{3,2,1,0:T(8,128)(2,1)} %copy-done.1, ...), custom_call_target="tpu_custom_call" | custom-call | tf_op jit(solution)/shard_map/trunk/pallas_call | solution.py:318
  30.1 7.9 %collective-permute-start.2 = (bf16[384,128]{1,0:T(8,128)(2,1)}, bf16[384,128]{1,0:T(8,128)(2,1)S(1)}, u32[]{:S(2)}, u32[]{:S(2)}) collective-permute-start(bf16[384,128]{1,0:T(8,128)(2,1)} %get-tuple-element.9), channel_id=1, source_target_pairs={{0,1},{1,0},{2,3},{3,2},{4,5},{5,4},{6,7},{7,6},{8,9},{9,8},{10,11... | collective-permute-start | bytes 294920 | tf_op jit(solution)/shard_map/ppermute | solution.py:340
  38.0 0.7 %collective-permute-start.3 = (bf16[384,128]{1,0:T(8,128)(2,1)}, bf16[384,128]{1,0:T(8,128)(2,1)S(1)}, u32[]{:S(2)}, u32[]{:S(2)}) collective-permute-start(bf16[384,128]{1,0:T(8,128)(2,1)} %get-tuple-element.10), channel_id=1, source_target_pairs={{1,2},{3,4},{5,6},{7,8},{9,10},{11,12},{13,14},{2,1},{4,3},{6,5},{... | collective-permute-start | bytes 294920 | tf_op jit(solution)/shard_map/ppermute | solution.py:339
  38.7 0.1 multiply_bitcast_fusion
  38.7 0.1 reshape.26
  38.8 0.6 pad.19.w_head
  39.4 0.0 collective-permute-done.2.from_pair
  39.4 0.0 copy-start.2
  39.5 0.0 collective-permute-done.3.from_next
  39.5 0.0 copy-start.3
  39.5 0.6 copy-done.2
  40.1 0.0 copy-done.3
  40.1 2.8 %tail.1 = bf16[32,1536]{1,0:T(8,128)(2,1)} custom-call(s32[3]{0:T(128)} %pad_add_fusion.flags, f32[4,32,16,128]{3,2,1,0:T(8,128)} %get-tuple-element.8.inner, bf16[384,128]{1,0:T(8,128)(2,1)} %copy-done.2, bf16[384,128]{1,0:T(8,128)(2,1)} %copy-done.3, bf16[16,192]{1,0:T(8,128)(2,1)} %pad.19.w_head, s32[1,32]{1,0:T(1,128)} %tissue.1, s32[1,32]{1,0:T(1,128)} %owners.1), custom_call_target="tpu_custom_call" | custom-call | tf_op jit(solution)/shard_map/tail/pallas_call | solution.py:341
  43.0 0.9 %reshape.27 = bf16[16,2,1536]{2,1,0:T(2,128)(2,1)S(1)} reshape(bf16[32,1536]{1,0:T(8,128)(2,1)} %tail.1) | data formatting | bytes 196608 | tf_op jit(solution)/shard_map/reshape | solution.py:352
  43.9 19.1 %all_to_all.5 = bf16[16,2,1536]{2,1,0:T(2,128)(2,1)S(1)} all-to-all(bf16[16,2,1536]{2,1,0:T(2,128)(2,1)S(1)} %reshape.27), channel_id=1, replica_groups=mesh['grp'=2,'gz'=16] {'gz'}, dimensions={0} | all-to-all | bytes 196608 | tf_op jit(solution)/shard_map/all_to_all | solution.py:353
  63.0 0.6 %copy.15 = bf16[1,16,2,1536]{3,2,1,0:T(2,128)(2,1)} copy(bf16[1,16,2,1536]{3,2,1,0:T(2,128)(2,1)S(1)} %bitcast.12) | data formatting | bytes 196608
  (6 shorter events, 0.1 us)
Async XLA Ops:
  0.0 2.3 %copy-start.5 = (bf16[48,324]{1,0:T(8,128)(2,1)S(1)}, bf16[48,324]{1,0:T(8,128)(2,1)}, u32[]{:S(2)}) copy-start(bf16[48,324]{1,0:T(8,128)(2,1)} %param.9) | copy-start | bytes 93316
  1.1 3.8 %collective-permute-start = (bf16[12,3,32,128]{3,2,1,0:T(8,128)(2,1)S(1)}, bf16[12,3,32,128]{3,2,1,0:T(8,128)(2,1)S(1)}, u32[]{:S(2)}, u32[]{:S(2)}) collective-permute-start(bf16[12,3,32,128]{3,2,1,0:T(8,128)(2,1)S(1)} %get-tuple-element.12), channel_id=1, source_target_pairs={{0,1},{1,0},{2,3},{3,2},{4,5},{5,4},{6,7},{7,6},{8,9},{9,8},{10,11... | collective-permute-start | bytes 884744 | tf_op jit(solution)/shard_map/ppermute | solution.py:303
  1.7 3.3 %collective-permute-start.1 = (bf16[12,3,32,128]{3,2,1,0:T(8,128)(2,1)S(1)}, bf16[12,3,32,128]{3,2,1,0:T(8,128)(2,1)S(1)}, u32[]{:S(2)}, u32[]{:S(2)}) collective-permute-start(bf16[12,3,32,128]{3,2,1,0:T(8,128)(2,1)S(1)} %get-tuple-element.11), channel_id=1, source_target_pairs={{1,2},{3,4},{5,6},{7,8},{9,10},{11,12},{13,14},{2,1},{4,3},{6,5},{... | collective-permute-start | bytes 884744 | tf_op jit(solution)/shard_map/ppermute | solution.py:302
  2.6 0.8 %copy-start.4 = (bf16[12,1296]{1,0:T(8,128)(2,1)S(1)}, bf16[12,1296]{1,0:T(8,128)(2,1)}, u32[]{:S(2)}) copy-start(bf16[12,1296]{1,0:T(8,128)(2,1)} %param.12) | copy-start | bytes 93316
  3.6 0.7 %copy-start.6 = (bf16[3,12]{1,0:T(4,128)(2,1)S(1)}, bf16[3,12]{1,0:T(4,128)(2,1)}, u32[]{:S(2)}) copy-start(bf16[3,12]{1,0:T(4,128)(2,1)} %param.13) | copy-start | bytes 220
  4.9 0.7 %copy-start = (bf16[12,3,32,128]{3,2,1,0:T(8,128)(2,1)}, bf16[12,3,32,128]{3,2,1,0:T(8,128)(2,1)S(1)}, u32[]{:S(2)}) copy-start(bf16[12,3,32,128]{3,2,1,0:T(8,128)(2,1)S(1)} %collective-permute-done.from_pair) | copy-start | bytes 884740
  5.0 0.8 %copy-start.1 = (bf16[12,3,32,128]{3,2,1,0:T(8,128)(2,1)}, bf16[12,3,32,128]{3,2,1,0:T(8,128)(2,1)S(1)}, u32[]{:S(2)}) copy-start(bf16[12,3,32,128]{3,2,1,0:T(8,128)(2,1)S(1)} %collective-permute-done.1.from_next) | copy-start | bytes 884740
  30.1 9.4 %collective-permute-start.2 = (bf16[384,128]{1,0:T(8,128)(2,1)}, bf16[384,128]{1,0:T(8,128)(2,1)S(1)}, u32[]{:S(2)}, u32[]{:S(2)}) collective-permute-start(bf16[384,128]{1,0:T(8,128)(2,1)} %get-tuple-element.9), channel_id=1, source_target_pairs={{0,1},{1,0},{2,3},{3,2},{4,5},{5,4},{6,7},{7,6},{8,9},{9,8},{10,11... | collective-permute-start | bytes 294920 | tf_op jit(solution)/shard_map/ppermute | solution.py:340
  38.0 1.4 %collective-permute-start.3 = (bf16[384,128]{1,0:T(8,128)(2,1)}, bf16[384,128]{1,0:T(8,128)(2,1)S(1)}, u32[]{:S(2)}, u32[]{:S(2)}) collective-permute-start(bf16[384,128]{1,0:T(8,128)(2,1)} %get-tuple-element.10), channel_id=1, source_target_pairs={{1,2},{3,4},{5,6},{7,8},{9,10},{11,12},{13,14},{2,1},{4,3},{6,5},{... | collective-permute-start | bytes 294920 | tf_op jit(solution)/shard_map/ppermute | solution.py:339
  39.4 0.6 %copy-start.2 = (bf16[384,128]{1,0:T(8,128)(2,1)}, bf16[384,128]{1,0:T(8,128)(2,1)S(1)}, u32[]{:S(2)}) copy-start(bf16[384,128]{1,0:T(8,128)(2,1)S(1)} %collective-permute-done.2.from_pair) | copy-start | bytes 294916
  39.5 0.7 %copy-start.3 = (bf16[384,128]{1,0:T(8,128)(2,1)}, bf16[384,128]{1,0:T(8,128)(2,1)S(1)}, u32[]{:S(2)}) copy-start(bf16[384,128]{1,0:T(8,128)(2,1)S(1)} %collective-permute-done.3.from_next) | copy-start | bytes 294916

commit v2 on v1

v2 whole, which is shorter than its diff:
```python
import jax
import jax.numpy as jnp
import numpy as np
from jax import lax
from jax.experimental import pallas as pl
from jax.experimental.pallas import tpu as pltpu
from jax.sharding import PartitionSpec as P

BY = 8
BX = 16
SEND_CAP = 2
HALO = 3
F32 = jnp.float32
BF16 = jnp.bfloat16


def iota(shape, dim):
    return lax.broadcasted_iota(jnp.int32, shape, dim)


def beside(value, width):
    lane = iota(value.shape, 1) % width
    left = jnp.where(lane == 0, jnp.zeros_like(value), pltpu.roll(value, 1, 1))
    right = jnp.where(
        lane == width - 1, jnp.zeros_like(value), pltpu.roll(value, value.shape[1] - 1, 1)
    )
    return left, value, right


def trunk_kernel(
    flags,
    features,
    from_pair,
    from_next,
    w_first,
    w_second,
    w_lift,
    w_edge,
    to_pair,
    to_next,
    cols_3,
    plain,
    cols_1,
    first,
    cols_2,
    border,
    edge,
):
    c0, depth, rows, lanes = features.shape
    c1, c2 = w_lift.shape
    half_rows = rows // 2
    wide = depth + 2 * HALO
    pairs = (wide - 2) // 2
    odd = flags[0]
    low_ok = flags[1]
    high_ok = flags[2]

    def face_at(z, c):
        return slice((z * c0 + c) * rows, (z * c0 + c + 1) * rows)

    for z in range(HALO):
        for c in range(c0):
            a = from_pair[c, z].astype(F32)
            b = from_next[c, z].astype(F32)
            plain[face_at(z, c)] = jnp.where(odd == 1, a, b)
            plain[face_at(HALO + depth + z, c)] = jnp.where(odd == 1, b, a)
    for z in range(depth):
        for c in range(c0):
            plain[face_at(HALO + z, c)] = features[c, z].astype(F32)

    group = 4 * c0
    pad_1 = jnp.zeros((3 * group, lanes), BF16)
    for p in range(pairs):
        cols_1[p, 0] = pad_1
        cols_1[p, rows + 1] = pad_1

    def spread_1(p, carry):
        for y in range(rows):
            face = plain[pl.ds(p * (2 * c0 * rows) + y, group, stride=rows), :]
            cols_1[p, y + 1] = jnp.concatenate(beside(face, lanes), axis=0).astype(BF16)
        return carry

    lax.fori_loop(0, pairs, spread_1, 0)

    weight_1 = w_first[...]
    run_1 = 16

    def conv_1(i, carry):
        p = i // (rows // run_1)
        y = (i % (rows // run_1)) * run_1
        x = jnp.concatenate(
            [
                jnp.concatenate([cols_1[p, y + b + j] for b in range(3)], axis=0)
                for j in range(run_1)
            ],
            axis=1,
        )
        out = jnp.dot(weight_1, x, preferred_element_type=F32)
        out = jnp.maximum(out, 0.0).astype(BF16)
        for j in range(run_1):
            for z in range(2):
                first[2 * p + z, y + j] = out[z * c1 : (z + 1) * c1, j * lanes : (j + 1) * lanes]
        return carry

    lax.fori_loop(0, pairs * (rows // run_1), conv_1, 0)

    pick = (iota((2 * lanes, lanes), 0) == 2 * iota((2 * lanes, lanes), 1)).astype(BF16)
    lane = iota((c1, lanes), 1)
    low_half = lane < lanes // 2
    keep_low = jnp.logical_or(jnp.logical_not(low_half), low_ok == 1)
    keep_high = jnp.logical_or(low_half, high_ok == 1)
    pad_2 = jnp.zeros((3 * c1, lanes), BF16)
    for a in range(3):
        cols_2[a, 0] = pad_2
        cols_2[a, half_rows + 1] = pad_2
    run_p = 4

    def pool(i, carry):
        y0 = i * run_p
        both = []
        for j in range(run_p):
            y = 2 * (y0 + j)
            tops = []
            for p in range(4):
                m = jnp.maximum(
                    jnp.maximum(first[2 * p, y], first[2 * p, y + 1]),
                    jnp.maximum(first[2 * p + 1, y], first[2 * p + 1, y + 1]),
                ).astype(F32)
                tops.append(jnp.maximum(m, pltpu.roll(m, lanes - 1, 1)).astype(BF16))
            both.append(jnp.concatenate([tops[0], tops[1]], axis=1))
            both.append(jnp.concatenate([tops[2], tops[3]], axis=1))
        packed = jnp.dot(jnp.concatenate(both, axis=0), pick, preferred_element_type=F32)
        for j in range(run_p):
            at = 2 * j * c1
            low = jnp.where(keep_low, packed[at : at + c1], 0.0)
            high = jnp.where(keep_high, packed[at + c1 : at + 2 * c1], 0.0)
            middle = pltpu.roll(jnp.where(low_half, high, low), lanes // 2, 1)
            for a, value in enumerate((low, middle, high)):
                value = jnp.concatenate(beside(value, lanes // 2), axis=0)
                cols_2[a, y0 + j + 1] = value.astype(BF16)
        return carry

    lax.fori_loop(0, half_rows // run_p, pool, 0)

    weight_2 = w_second[...]
    weight_l = w_lift[...]
    widen = (iota((lanes, 2 * lanes), 0) == iota((lanes, 2 * lanes), 1) // 2).astype(BF16)
    run_2 = 4

    def conv_2(i, carry):
        y = i * run_2
        x = jnp.concatenate(
            [
                jnp.concatenate(
                    [cols_2[a, y + b + j] for a in range(3) for b in range(3)], axis=0
                )
                for j in range(run_2)
            ],
            axis=1,
        )
        second = jnp.dot(weight_2, x, preferred_element_type=F32)
        second = jnp.maximum(second, 0.0).astype(BF16)
        stacked = jnp.concatenate(
            [second[:, j * lanes : (j + 1) * lanes] for j in range(run_2)], axis=0
        )
        stacked = jnp.dot(stacked, widen, preferred_element_type=F32).astype(BF16)
        spread = jnp.concatenate(
            [stacked[j * c2 : (j + 1) * c2] for j in range(run_2)], axis=1
        )
        lifted = jnp.dot(weight_l, spread, preferred_element_type=F32)
        for j in range(run_2):
            for zz in range(2):
                at = (2 * j + zz) * lanes
                value = lifted[:, at : at + lanes]
                for dz in range(2):
                    for dy in range(2):
                        z = 2 * zz + dz
                        row = 2 * (y + j) + dy
                        merged = value + first[z + 2, row].astype(F32)
                        merged = merged.astype(BF16).astype(F32)
                        cols_3[z, row] = jnp.concatenate(beside(merged, lanes), axis=0).astype(
                            BF16
                        )
        return carry

    lax.fori_loop(0, half_rows // run_2, conv_2, 0)

    cu = edge.shape[0] // rows
    border[...] = jnp.zeros_like(border)
    weight_e = w_edge[...]
    run_e = 8

    def conv_e(i, carry):
        y = i * run_e
        x = jnp.concatenate(
            [
                jnp.concatenate([cols_3[0, y + j], cols_3[depth - 1, y + j]], axis=0)
                for j in range(run_e)
            ],
            axis=1,
        )
        out = jnp.dot(weight_e, x, preferred_element_type=F32)
        for k, term in row_sums(out, run_e, 2 * cu, lanes):
            border[y + k] += term
        return carry

    lax.fori_loop(0, rows // run_e, conv_e, 0)

    for target, upward in ((to_pair, odd == 0), (to_next, odd == 1)):
        for y in range(rows):
            down = border[y + 1, 0:cu]
            up = border[y + 1, cu : 2 * cu]
            edge[y * cu : (y + 1) * cu] = jnp.where(upward, up, down)
        target[...] = edge[...].astype(BF16)


def row_sums(out, run, height, lanes):
    for k in range(run + 2):
        term = None
        for b in range(3):
            j = k - 2 + b
            if 0 <= j < run:
                value = out[b * height : (b + 1) * height, j * lanes : (j + 1) * lanes]
                term = value if term is None else term + value
        yield k, term


def inner_kernel(cols_3, w_inner, inner):
    depth, rows, _, lanes = cols_3.shape
    height = inner.shape[2]
    run = 8
    for q in range(2):
        inner[q, 0] = jnp.zeros((height, lanes), F32)
        inner[q, 1] = jnp.zeros((height, lanes), F32)
        weight = w_inner[q]

        def conv_3(i, carry, q=q, weight=weight):
            y = i * run
            x = jnp.concatenate(
                [
                    jnp.concatenate([cols_3[q + a, y + j] for a in range(3)], axis=0)
                    for j in range(run)
                ],
                axis=1,
            )
            out = jnp.dot(weight, x, preferred_element_type=F32)
            for k, term in row_sums(out, run, height, lanes):
                if k < 2:
                    inner[q, y + k] += term
                else:
                    inner[q, y + k] = term
            return carry

        lax.fori_loop(0, rows // run, conv_3, 0)


def tail_kernel(flags, inner, from_pair, from_next, w_head, tissue, owners, out, edge, shown):
    depth = 4
    height, lanes = inner.shape[2:]
    rows = inner.shape[1] - 2
    cu = from_pair.shape[0] // rows
    odd = flags[0]
    a = from_pair[...].astype(F32)
    b = from_next[...].astype(F32)
    edge[0] = jnp.where(odd == 1, a, b)
    edge[1] = jnp.where(odd == 1, b, a)
    head = w_head[...]
    gap = jnp.zeros((height - cu, lanes), F32)
    run = 8
    for y0 in range(0, rows, run):
        columns = []
        for y in range(y0, y0 + run):
            parts = []
            value = jnp.concatenate(
                [
                    inner[q, y + 1]
                    + jnp.concatenate([edge[q, y * cu : (y + 1) * cu], gap], axis=0)
                    for q in range(2)
                ],
                axis=0,
            )
            value = jnp.maximum(value, 0.0)
            for _ in range(3):
                part = value.astype(BF16)
                parts.append(part)
                value = value - part.astype(F32)
            columns.append(jnp.concatenate(parts, axis=0))
        logits = jnp.dot(head, jnp.concatenate(columns, axis=1), preferred_element_type=F32)
        chance = jax.nn.sigmoid(logits)
        for j in range(run):
            shown[(y0 + j) * 16 : (y0 + j + 1) * 16] = chance[:, j * lanes : (j + 1) * lanes]

    sub = iota((BY, lanes), 0)
    group = iota((BY, lanes), 1) // BX
    faces = 3 * depth
    tiles = []
    for f in range(faces):
        blocks = []
        for by in range(rows // BY):
            v = shown[pl.ds(by * BY * 16 + f, BY, stride=16), :]
            for k in (1, 2, 4):
                s_bit = (sub // k) % 2
                g_bit = (group // k) % 2
                down = pltpu.roll(pltpu.roll(v, BY - k, 0), k * BX, 1)
                up = pltpu.roll(pltpu.roll(v, k, 0), lanes - k * BX, 1)
                v = jnp.where(s_bit == g_bit, v, jnp.where(s_bit < g_bit, down, up))
            blocks.append(v)
        tiles.append(jnp.concatenate(blocks, axis=0))
    tiles = jnp.concatenate(tiles, axis=1).astype(BF16)

    count = tissue.shape[1]
    slots = out.shape[0]
    own = jnp.broadcast_to(owners[...], (count, count))
    seen = jnp.broadcast_to(tissue[...], (count, count))
    r = iota((count, count), 0)
    c = iota((count, count), 1)
    own_column = jnp.sum(jnp.where(r == c, own, 0), axis=1, keepdims=True)
    seen_column = jnp.sum(jnp.where(r == c, seen, 0), axis=1, keepdims=True)
    before = jnp.where(jnp.logical_and(own_column == own, r < c), 1, 0)
    slot = owners[...] * SEND_CAP + jnp.sum(before, axis=0, keepdims=True)
    slot_pick = (iota((slots, count), 0) == slot).astype(F32).astype(BF16)
    blocks = tiles.shape[0]
    block_pick = (seen_column == iota((count, blocks), 1)).astype(F32).astype(BF16)
    select = jnp.dot(slot_pick, block_pick, preferred_element_type=F32).astype(BF16)
    out[...] = jnp.dot(select, tiles, preferred_element_type=F32).astype(BF16)


def on_device(features, w_first, w_second, w_lift, w_merge, w_affine, tissue, owners):
    c0, depth, rows, lanes = features.shape
    c1, c2 = w_lift.shape
    cu = w_merge.shape[0]
    devices = lax.axis_size("gz")
    here = lax.axis_index("gz")
    odd = here % 2
    flags = jnp.stack([odd, (here > 0).astype(jnp.int32), (here < devices - 1).astype(jnp.int32)])
    pair = [(i, i ^ 1) for i in range(devices)]
    after = [(i, i + 1) for i in range(1, devices - 1, 2)]
    after = after + [(j, i) for i, j in after]

    lower = lax.slice_in_dim(features, 0, HALO, axis=1)
    upper = lax.slice_in_dim(features, depth - HALO, depth, axis=1)
    from_next = lax.ppermute(jnp.where(odd == 1, upper, lower), "gz", after)
    from_pair = lax.ppermute(jnp.where(odd == 1, lower, upper), "gz", pair)

    taps = w_first.reshape(c1, 3, 3, 3, c0).transpose(0, 2, 3, 1, 4)
    taps = jnp.stack(
        [jnp.pad(taps, ((0, 0),) * 3 + ((z, 1 - z), (0, 0))) for z in range(2)]
    ).reshape(2 * c1, 36 * c0)

    merge = w_merge.reshape(cu, 3, 3, 3 * c1).transpose(1, 2, 0, 3)
    none = jnp.zeros_like(merge[0])

    def arrange(table):
        table = [[none if a is None else merge[a] for a in line] for line in table]
        whole = jnp.stack([jnp.concatenate(line, axis=2) for line in table], axis=1)
        return whole.reshape(3 * len(table) * cu, -1)

    w_edge = arrange([[2, None], [None, 0]])
    w_inner = jnp.stack(
        [arrange([[1, 2, None], [0, 1, 2]]), arrange([[None, 0, 1], [0, 1, 2]])]
    )
    place = jnp.asarray(np.eye(4)[:, [0, 1, 3, 2]], w_affine.dtype)
    head = w_affine[:, None, None, :] * place[None, :, :, None]
    head = jnp.tile(head.reshape(3 * depth, depth * cu), (1, 3))
    head = jnp.pad(head, ((0, 16 - 3 * depth), (0, 0)))
    taps, w_edge, w_inner, head = lax.optimization_barrier((taps, w_edge, w_inner, head))

    vmem = pl.BlockSpec(memory_space=pltpu.VMEM)
    smem = pl.BlockSpec(memory_space=pltpu.SMEM)
    shape = jax.ShapeDtypeStruct
    wide = depth + 2 * HALO
    to_pair, to_next, cols_3 = pl.pallas_call(
        trunk_kernel,
        out_shape=(
            shape((rows * cu, lanes), BF16),
            shape((rows * cu, lanes), BF16),
            shape((depth, rows, 3 * c1, lanes), BF16),
        ),
        in_specs=[smem] + [vmem] * 7,
        out_specs=(vmem,) * 3,
        scratch_shapes=[
            pltpu.VMEM((wide * c0 * rows, lanes), F32),
            pltpu.VMEM((wide // 2 - 1, rows + 2, 12 * c0, lanes), BF16),
            pltpu.VMEM((wide - 2, rows, c1, lanes), BF16),
            pltpu.VMEM((3, rows // 2 + 2, 3 * c1, lanes), BF16),
            pltpu.VMEM((rows + 2, 2 * cu, lanes), F32),
            pltpu.VMEM((rows * cu, lanes), F32),
        ],
        compiler_params=pltpu.CompilerParams(vmem_limit_bytes=24 * 2**20),
        name="trunk",
    )(flags, features, from_pair, from_next, taps, w_second, w_lift, w_edge)

    edge_next = lax.ppermute(to_next, "gz", after)
    edge_pair = lax.ppermute(to_pair, "gz", pair)
    inner = pl.pallas_call(
        inner_kernel,
        out_shape=shape((2, rows + 2, 2 * cu, lanes), F32),
        in_specs=[vmem] * 2,
        out_specs=vmem,
        compiler_params=pltpu.CompilerParams(vmem_limit_bytes=16 * 2**20),
        cost_estimate=pl.CostEstimate(
            flops=2 * 27 * c1 * cu * depth * rows * lanes,
            bytes_accessed=8 * 2**20,
            transcendentals=0,
        ),
        name="inner",
    )(cols_3, w_inner)
    outgoing = pl.pallas_call(
        tail_kernel,
        out_shape=shape((devices * SEND_CAP, 3 * depth * BY * BX), BF16),
        in_specs=[smem] + [vmem] * 6,
        out_specs=vmem,
        scratch_shapes=[
            pltpu.VMEM((2, rows * cu, lanes), F32),
            pltpu.VMEM((rows * 16, lanes), F32),
        ],
        compiler_params=pltpu.CompilerParams(vmem_limit_bytes=8 * 2**20),
        name="tail",
    )(flags, inner, edge_pair, edge_next, head, tissue, owners)
    outgoing = outgoing.reshape(devices, SEND_CAP, -1)
    return lax.all_to_all(outgoing, "gz", split_axis=0, concat_axis=0, tiled=True)[None]


def solution(mesh):
    placed = (
        P(None, ("grp", "gz"), None, None),
        P(),
        P(),
        P(),
        P(),
        P(),
        P(("grp", "gz"), None),
        P(("grp", "gz"), None),
    )
    return jax.shard_map(
        on_device,
        mesh=mesh,
        in_specs=placed,
        out_specs=P(("grp", "gz"), None, None, None),
        check_vma=False,
    )
```

time: 64 us -> 48.4 us (0.76)
  Pallas kernels: 27.1 us -> 16.6 us
  local copies, waits for them, and re-layouts: 5.7 us -> 3.46 us
  blocking collectives: 19.1 us -> 17 us
  starting transfers between devices: 9.82 us -> 8.52 us
    pallas_call x1 -> x2, Pallas kernels: 24.3 us -> 15.3 us  [the longest x1 13.1 us: on_device(): pl.pallas_call(trunk_kernel, out_shape=(shape((rows * cu, lanes), BF16),...]
    ppermute x1, starting transfers between devices: 7.94 us -> 2.76 us  [on_device(): edge_pair = lax.ppermute(to_pair, 'gz', pair)]
    ppermute x1, starting transfers between devices: 0.56 us -> 4.42 us  [on_device(): from_pair = lax.ppermute(jnp.where(odd == 1, lower, upper), 'gz', pair)]
    all_to_all x1, blocking collectives: 19.1 us -> 17 us  [on_device(): lax.all_to_all(outgoing, 'gz', split_axis=0, concat_axis=0, tiled=True)]
    pallas_call x1, Pallas kernels: 2.85 us -> 1.32 us  [on_device(): pl.pallas_call(tail_kernel, out_shape=shape((devices * SEND_CAP, 3 * dept...]
    pad x4 -> x1, local copies, waits for them, and re-layouts: 1.29 us -> 0.01 us  [on_device(): head = jnp.pad(head, ((0, 16 - 3 * depth), (0, 0)))]
    reshape x1, local copies, waits for them, and re-layouts: 0.93 us -> 0.04 us  [on_device(): outgoing = outgoing.reshape(devices, SEND_CAP, -1)]
    unnamed x17 -> x12, local copies, waits for them, and re-layouts: 2.36 us -> 1.55 us
  transfers between devices with their start and end apart: 4 -> 4, of which waited for: 0 -> 0; matrix products, arithmetic and copies ran while one was open for 5% -> 8% of each run, Pallas kernels for 0% -> 5%
where the time goes in v2:
time: 48.4 us; the launch traced here: 48.1 us
  blocking collectives  17 us (35%)
  Pallas kernels  16.6 us (34%)
  starting transfers between devices  8.52 us (18%)
  local copies, waits for them, and re-layouts  3.46 us (7%)
  other arithmetic  2.29 us (5%)
    all_to_all x1, blocking collectives, on_device(): lax.all_to_all(outgoing, 'gz', split_axis=0, concat_axis=0, tiled=True)  17 us
    pallas_call x1, Pallas kernels, on_device(): pl.pallas_call(trunk_kernel, out_shape=(shape((rows * cu, lanes), BF16),...  13.1 us
    ppermute x1, starting transfers between devices, on_device(): from_pair = lax.ppermute(jnp.where(odd == 1, lower, upper), 'gz', pair)  4.42 us
    ppermute x1, starting transfers between devices, on_device(): edge_pair = lax.ppermute(to_pair, 'gz', pair)  2.76 us
    pallas_call x1, Pallas kernels, on_device(): pl.pallas_call(inner_kernel, out_shape=shape((2, rows + 2, 2 * cu, lanes)...  2.2 us
    unnamed x12, local copies, waits for them, and re-layouts  1.55 us
    pallas_call x1, Pallas kernels, on_device(): pl.pallas_call(tail_kernel, out_shape=shape((devices * SEND_CAP, 3 * dept...  1.32 us
    select_n x1, other arithmetic, on_device(): from_next = lax.ppermute(jnp.where(odd == 1, upper, lower), 'gz', after)  1.16 us
  transfers between devices with their start and end apart: 4, of which 0 were waited for; matrix products, arithmetic and copies ran while one was open for 8% of the time, Pallas kernels for 5%

profile of v2, /device:TPU:0, one launch (start us, length us, event | category | flops | bytes accessed | tf_op | source)
XLA Modules:
  0.0 48.1 jit_solution(14024494985886919579)
XLA Ops:
  0.0 0.0 copy-start
  0.0 0.0 copy-start.2
  0.0 0.0 copy-start.1
  0.0 1.2 %broadcast_select_fusion = (bf16[12,3,32,128]{3,2,1,0:T(8,128)(2,1)S(1)}, bf16[12,3,32,128]{3,2,1,0:T(8,128)(2,1)S(1)}) fusion(pred[]{:T(512)S(6)} %eq.6, bf16[12,4,32,128]{3,2,1,0:T(8,128)(2,1)} %features.1), kind=kLoop, calls=%fused_computation.1 | loop fusion | flops 294912 | bytes 1179649 | tf_op jit(solution)/shard_map/jit(_where)/select_n | solution.py:342
  1.2 0.7 %collective-permute-start.1 = (bf16[12,3,32,128]{3,2,1,0:T(8,128)(2,1)S(1)}, bf16[12,3,32,128]{3,2,1,0:T(8,128)(2,1)S(1)}, u32[]{:S(2)}, u32[]{:S(2)}) collective-permute-start(bf16[12,3,32,128]{3,2,1,0:T(8,128)(2,1)S(1)} %get-tuple-element.19), channel_id=1, source_target_pairs={{1,2},{3,4},{5,6},{7,8},{9,10},{11,12},{13,14},{2,1},{4,3},{6,5},{... | collective-permute-start | bytes 884744 | tf_op jit(solution)/shard_map/ppermute | solution.py:342
  1.9 4.4 %collective-permute-start = (bf16[12,3,32,128]{3,2,1,0:T(8,128)(2,1)S(1)}, bf16[12,3,32,128]{3,2,1,0:T(8,128)(2,1)S(1)}, u32[]{:S(2)}, u32[]{:S(2)}) collective-permute-start(bf16[12,3,32,128]{3,2,1,0:T(8,128)(2,1)S(1)} %get-tuple-element.20), channel_id=1, source_target_pairs={{0,1},{1,0},{2,3},{3,2},{4,5},{5,4},{6,7},{7,6},{8,9},{9,8},{10,11... | collective-permute-start | bytes 884744 | tf_op jit(solution)/shard_map/ppermute | solution.py:343
  6.3 0.8 %broadcast_multiply_fusion = bf16[3,4,4,12]{3,2,1,0:T(4,128)(2,1)S(1)} fusion(bf16[4,4]{1,0:T(4,128)(2,1)} %constant.26.clone, bf16[3,12]{1,0:T(4,128)(2,1)} %param.14), kind=kLoop, calls=%fused_computation.18 | loop fusion | flops 576 | bytes 1256 | tf_op jit(solution)/shard_map/mul | solution.py:363
  7.1 0.1 mul.23
  7.2 0.1 tile.9
  7.2 0.9 %reshape.36 = bf16[12,3,3,144]{3,2,1,0:T(4,128)(2,1)S(1)} reshape(bf16[12,1296]{1,0:T(8,128)(2,1)} %param.13) | data formatting | bytes 62208 | tf_op jit(solution)/shard_map/reshape | solution.py:350
  8.2 0.1 pad_bitcast_fusion.2
  8.4 0.1 maximum_bitcast_fusion
  8.6 0.9 %copy.14 = bf16[48,324]{0,1:T(8,128)(2,1)S(1)} copy(bf16[48,324]{1,0:T(8,128)(2,1)} %param.10) | data formatting | bytes 62208 | tf_op args[1]
  9.6 0.0 copy-start.3
  9.6 0.0 copy-start.4
  9.6 0.1 pad_maximum_fusion
  9.7 0.2 copy.15
  9.9 0.1 reshape.35
  10.1 0.1 copy.19.w_first
  10.2 0.1 pad_add_fusion.flags
  10.3 0.0 collective-permute-done.1.from_next
  10.3 0.0 collective-permute-done.from_pair
  10.3 0.0 copy-done
  10.3 0.0 copy-done.2
  10.3 0.0 copy-done.1
  10.3 13.1 %trunk.1 = (bf16[384,128]{1,0:T(8,128)(2,1)S(1)}, bf16[384,128]{1,0:T(8,128)(2,1)S(1)}, bf16[4,32,144,128]{3,2,1,0:T(8,128)(2,1)S(1)}) custom-call(s32[3]{0:T(128)S(1)} %pad_add_fusion.flags, bf16[12,4,32,128]{3,2,1,0:T(8,128)(2,1)S(1)} %copy-done, bf16[12,3,32,128]{3,2,1,0:T(8,128)(2,1)S(1)} %collective-permute-done.from_pair, ...), custom_call_target="tpu_custom_call" | custom-call | tf_op jit(solution)/shard_map/trunk/pallas_call | solution.py:372
  23.4 2.8 %collective-permute-start.2 = (bf16[384,128]{1,0:T(8,128)(2,1)S(1)}, bf16[384,128]{1,0:T(8,128)(2,1)S(1)}, u32[]{:S(2)}, u32[]{:S(2)}) collective-permute-start(bf16[384,128]{1,0:T(8,128)(2,1)S(1)} %get-tuple-element.16), channel_id=1, source_target_pairs={{0,1},{1,0},{2,3},{3,2},{4,5},{5,4},{6,7},{7,6},{8,9},{9,8},{10,11... | collective-permute-start | bytes 294920 | tf_op jit(solution)/shard_map/ppermute | solution.py:394
  26.2 0.7 %collective-permute-start.3 = (bf16[384,128]{1,0:T(8,128)(2,1)S(1)}, bf16[384,128]{1,0:T(8,128)(2,1)S(1)}, u32[]{:S(2)}, u32[]{:S(2)}) collective-permute-start(bf16[384,128]{1,0:T(8,128)(2,1)S(1)} %get-tuple-element.17), channel_id=1, source_target_pairs={{1,2},{3,4},{5,6},{7,8},{9,10},{11,12},{13,14},{2,1},{4,3},{6,5},{... | collective-permute-start | bytes 294920 | tf_op jit(solution)/shard_map/ppermute | solution.py:393
  26.9 2.2 %inner.1 = f32[2,34,24,128]{3,2,1,0:T(8,128)S(1)} custom-call(bf16[4,32,144,128]{3,2,1,0:T(8,128)(2,1)S(1)} %get-tuple-element.14.cols_3, bf16[2,72,432]{2,1,0:T(8,128)(2,1)S(1)} %pad_maximum_fusion.1.w_inner), custom_call_target="tpu_custom_call" | custom-call | flops 509607936 | bytes 8388608 | tf_op jit(solution)/shard_map/inner/pallas_call | solution.py:395
  29.1 0.0 collective-permute-done.2.from_pair
  29.1 0.0 collective-permute-done.3.from_next
  29.1 0.0 copy-done.3
  29.1 0.0 copy-done.4
  29.1 1.3 %tail.1 = bf16[32,1536]{1,0:T(8,128)(2,1)S(1)} custom-call(s32[3]{0:T(128)S(1)} %pad_add_fusion.flags, f32[2,34,24,128]{3,2,1,0:T(8,128)S(1)} %inner.1, bf16[384,128]{1,0:T(8,128)(2,1)S(1)} %collective-permute-done.2.from_pair, bf16[384,128]{1,0:T(8,128)(2,1)S(1)} %collective-permute-done.3.from_next, bf16[16,144]{1,0:T(8,128)(2,1)S(1)} %pad.16.w_head, ...), custom_call_target="tpu_custom_call" | custom-call | tf_op jit(solution)/shard_map/tail/pallas_call | solution.py:408
  30.5 17.0 %all_to_all.5 = bf16[16,2,1536]{2,1,0:T(2,128)(2,1)S(1)} all-to-all(bf16[16,2,1536]{2,1,0:T(2,128)(2,1)S(1)} %reshape.38), channel_id=1, replica_groups=mesh['grp'=2,'gz'=16] {'gz'}, dimensions={0} | all-to-all | bytes 196608 | tf_op jit(solution)/shard_map/all_to_all | solution.py:421
  47.5 0.6 %copy.23 = bf16[1,16,2,1536]{3,2,1,0:T(2,128)(2,1)} copy(bf16[1,16,2,1536]{3,2,1,0:T(2,128)(2,1)S(1)} %bitcast.35) | data formatting | bytes 196608
  (15 shorter events, 0.3 us)
Async XLA Ops:
  0.0 10.3 %copy-start = (bf16[12,4,32,128]{3,2,1,0:T(8,128)(2,1)S(1)}, bf16[12,4,32,128]{3,2,1,0:T(8,128)(2,1)}, u32[]{:S(2)}) copy-start(bf16[12,4,32,128]{3,2,1,0:T(8,128)(2,1)} %features.1) | copy-start | bytes 1179652
  0.0 10.3 %copy-start.2 = (bf16[48,96]{1,0:T(8,128)(2,1)S(1)}, bf16[48,96]{1,0:T(8,128)(2,1)}, u32[]{:S(2)}) copy-start(bf16[48,96]{1,0:T(8,128)(2,1)} %w_lift.1) | copy-start | bytes 27652
  0.0 10.3 %copy-start.1 = (bf16[96,1296]{1,0:T(8,128)(2,1)S(1)}, bf16[96,1296]{1,0:T(8,128)(2,1)}, u32[]{:S(2)}) copy-start(bf16[96,1296]{1,0:T(8,128)(2,1)} %w_second.1) | copy-start | bytes 746500
  1.2 9.1 %collective-permute-start.1 = (bf16[12,3,32,128]{3,2,1,0:T(8,128)(2,1)S(1)}, bf16[12,3,32,128]{3,2,1,0:T(8,128)(2,1)S(1)}, u32[]{:S(2)}, u32[]{:S(2)}) collective-permute-start(bf16[12,3,32,128]{3,2,1,0:T(8,128)(2,1)S(1)} %get-tuple-element.19), channel_id=1, source_target_pairs={{1,2},{3,4},{5,6},{7,8},{9,10},{11,12},{13,14},{2,1},{4,3},{6,5},{... | collective-permute-start | bytes 884744 | tf_op jit(solution)/shard_map/ppermute | solution.py:342
  1.9 8.5 %collective-permute-start = (bf16[12,3,32,128]{3,2,1,0:T(8,128)(2,1)S(1)}, bf16[12,3,32,128]{3,2,1,0:T(8,128)(2,1)S(1)}, u32[]{:S(2)}, u32[]{:S(2)}) collective-permute-start(bf16[12,3,32,128]{3,2,1,0:T(8,128)(2,1)S(1)} %get-tuple-element.20), channel_id=1, source_target_pairs={{0,1},{1,0},{2,3},{3,2},{4,5},{5,4},{6,7},{7,6},{8,9},{9,8},{10,11... | collective-permute-start | bytes 884744 | tf_op jit(solution)/shard_map/ppermute | solution.py:343
  9.6 19.5 %copy-start.3 = (s32[1,32]{1,0:T(1,128)S(1)}, s32[1,32]{1,0:T(1,128)}, u32[]{:S(2)}) copy-start(s32[1,32]{1,0:T(1,128)} %tissue.1) | copy-start | bytes 388
  9.6 19.5 %copy-start.4 = (s32[1,32]{1,0:T(1,128)S(1)}, s32[1,32]{1,0:T(1,128)}, u32[]{:S(2)}) copy-start(s32[1,32]{1,0:T(1,128)} %owners.1) | copy-start | bytes 388
  23.4 5.6 %collective-permute-start.2 = (bf16[384,128]{1,0:T(8,128)(2,1)S(1)}, bf16[384,128]{1,0:T(8,128)(2,1)S(1)}, u32[]{:S(2)}, u32[]{:S(2)}) collective-permute-start(bf16[384,128]{1,0:T(8,128)(2,1)S(1)} %get-tuple-element.16), channel_id=1, source_target_pairs={{0,1},{1,0},{2,3},{3,2},{4,5},{5,4},{6,7},{7,6},{8,9},{9,8},{10,11... | collective-permute-start | bytes 294920 | tf_op jit(solution)/shard_map/ppermute | solution.py:394
  26.2 2.9 %collective-permute-start.3 = (bf16[384,128]{1,0:T(8,128)(2,1)S(1)}, bf16[384,128]{1,0:T(8,128)(2,1)S(1)}, u32[]{:S(2)}, u32[]{:S(2)}) collective-permute-start(bf16[384,128]{1,0:T(8,128)(2,1)S(1)} %get-tuple-element.17), channel_id=1, source_target_pairs={{1,2},{3,4},{5,6},{7,8},{9,10},{11,12},{13,14},{2,1},{4,3},{6,5},{... | collective-permute-start | bytes 294920 | tf_op jit(solution)/shard_map/ppermute | solution.py:393

commit v3 on v2

--- a/solution.py
+++ b/solution.py
@@ -55,8 +55,9 @@
     low_ok = flags[1]
     high_ok = flags[2]
 
+    pitch = plain.shape[0] // (wide * c0)
     def face_at(z, c):
-        return slice((z * c0 + c) * rows, (z * c0 + c + 1) * rows)
+        return slice((z * c0 + c) * pitch, (z * c0 + c) * pitch + rows)
 
     for z in range(HALO):
         for c in range(c0):
@@ -76,8 +77,8 @@
 
     def spread_1(p, carry):
         for y in range(rows):
-            face = plain[pl.ds(p * (2 * c0 * rows) + y, group, stride=rows), :]
-            cols_1[p, y + 1] = jnp.concatenate(beside(face, lanes), axis=0).astype(BF16)
+            face = plain[pl.ds(p * (2 * c0 * pitch) + y, group, stride=pitch), :]
+            cols_1[p, y + 1] = jnp.concatenate(beside(face.astype(BF16), lanes), axis=0)
         return carry
 
     lax.fori_loop(0, pairs, spread_1, 0)
@@ -102,7 +103,7 @@
                 first[2 * p + z, y + j] = out[z * c1 : (z + 1) * c1, j * lanes : (j + 1) * lanes]
         return carry
 
-    lax.fori_loop(0, pairs * (rows // run_1), conv_1, 0)
+    lax.fori_loop(0, pairs * (rows // run_1), conv_1, 0, unroll=4)
 
     pick = (iota((2 * lanes, lanes), 0) == 2 * iota((2 * lanes, lanes), 1)).astype(BF16)
     lane = iota((c1, lanes), 1)
@@ -114,6 +115,7 @@
         cols_2[a, 0] = pad_2
         cols_2[a, half_rows + 1] = pad_2
     run_p = 4
+    zero_2 = jnp.zeros((c1, lanes), BF16)
 
     def pool(i, carry):
         y0 = i * run_p
@@ -125,22 +127,21 @@
                 m = jnp.maximum(
                     jnp.maximum(first[2 * p, y], first[2 * p, y + 1]),
                     jnp.maximum(first[2 * p + 1, y], first[2 * p + 1, y + 1]),
-                ).astype(F32)
-                tops.append(jnp.maximum(m, pltpu.roll(m, lanes - 1, 1)).astype(BF16))
+                )
+                tops.append(jnp.maximum(m, pltpu.roll(m, lanes - 1, 1)))
             both.append(jnp.concatenate([tops[0], tops[1]], axis=1))
             both.append(jnp.concatenate([tops[2], tops[3]], axis=1))
-        packed = jnp.dot(jnp.concatenate(both, axis=0), pick, preferred_element_type=F32)
+        packed = jnp.dot(jnp.concatenate(both, axis=0), pick, preferred_element_type=F32).astype(BF16)
         for j in range(run_p):
             at = 2 * j * c1
-            low = jnp.where(keep_low, packed[at : at + c1], 0.0)
-            high = jnp.where(keep_high, packed[at + c1 : at + 2 * c1], 0.0)
+            low = jnp.where(keep_low, packed[at : at + c1], zero_2)
+            high = jnp.where(keep_high, packed[at + c1 : at + 2 * c1], zero_2)
             middle = pltpu.roll(jnp.where(low_half, high, low), lanes // 2, 1)
             for a, value in enumerate((low, middle, high)):
-                value = jnp.concatenate(beside(value, lanes // 2), axis=0)
-                cols_2[a, y0 + j + 1] = value.astype(BF16)
+                cols_2[a, y0 + j + 1] = jnp.concatenate(beside(value, lanes // 2), axis=0)
         return carry
 
-    lax.fori_loop(0, half_rows // run_p, pool, 0)
+    lax.fori_loop(0, half_rows // run_p, pool, 0, unroll=4)
 
     weight_2 = w_second[...]
     weight_l = w_lift[...]
@@ -177,13 +178,11 @@
                         z = 2 * zz + dz
                         row = 2 * (y + j) + dy
                         merged = value + first[z + 2, row].astype(F32)
-                        merged = merged.astype(BF16).astype(F32)
-                        cols_3[z, row] = jnp.concatenate(beside(merged, lanes), axis=0).astype(
-                            BF16
-                        )
+                        merged = merged.astype(BF16)
+                        cols_3[z, row] = jnp.concatenate(beside(merged, lanes), axis=0)
         return carry
 
-    lax.fori_loop(0, half_rows // run_2, conv_2, 0)
+    lax.fori_loop(0, half_rows // run_2, conv_2, 0, unroll=4)
 
     cu = edge.shape[0] // rows
     border[...] = jnp.zeros_like(border)
@@ -204,7 +203,7 @@
             border[y + k] += term
         return carry
 
-    lax.fori_loop(0, rows // run_e, conv_e, 0)
+    lax.fori_loop(0, rows // run_e, conv_e, 0, unroll=4)
 
     for target, upward in ((to_pair, odd == 0), (to_next, odd == 1)):
         for y in range(rows):
@@ -251,7 +250,7 @@
                     inner[q, y + k] = term
             return carry
 
-        lax.fori_loop(0, rows // run, conv_3, 0)
+        lax.fori_loop(0, rows // run, conv_3, 0, unroll=4)
 
 
 def tail_kernel(flags, inner, from_pair, from_next, w_head, tissue, owners, out, edge, shown):
@@ -288,7 +287,7 @@
         logits = jnp.dot(head, jnp.concatenate(columns, axis=1), preferred_element_type=F32)
         chance = jax.nn.sigmoid(logits)
         for j in range(run):
-            shown[(y0 + j) * 16 : (y0 + j + 1) * 16] = chance[:, j * lanes : (j + 1) * lanes]
+            shown[(y0 + j) * 24 : (y0 + j) * 24 + 16] = chance[:, j * lanes : (j + 1) * lanes]
 
     sub = iota((BY, lanes), 0)
     group = iota((BY, lanes), 1) // BX
@@ -297,7 +296,7 @@
     for f in range(faces):
         blocks = []
         for by in range(rows // BY):
-            v = shown[pl.ds(by * BY * 16 + f, BY, stride=16), :]
+            v = shown[pl.ds(by * BY * 24 + f, BY, stride=24), :]
             for k in (1, 2, 4):
                 s_bit = (sub // k) % 2
                 g_bit = (group // k) % 2
@@ -379,7 +378,7 @@
         in_specs=[smem] + [vmem] * 7,
         out_specs=(vmem,) * 3,
         scratch_shapes=[
-            pltpu.VMEM((wide * c0 * rows, lanes), F32),
+            pltpu.VMEM((wide * c0 * (rows + 8), lanes), F32),
             pltpu.VMEM((wide // 2 - 1, rows + 2, 12 * c0, lanes), BF16),
             pltpu.VMEM((wide - 2, rows, c1, lanes), BF16),
             pltpu.VMEM((3, rows // 2 + 2, 3 * c1, lanes), BF16),
@@ -412,7 +411,7 @@
         out_specs=vmem,
         scratch_shapes=[
             pltpu.VMEM((2, rows * cu, lanes), F32),
-            pltpu.VMEM((rows * 16, lanes), F32),
+            pltpu.VMEM((rows * 24, lanes), F32),
         ],
         compiler_params=pltpu.CompilerParams(vmem_limit_bytes=8 * 2**20),
         name="tail",

time: 48.4 us -> 43.3 us (0.89)
  Pallas kernels: 16.6 us -> 10.6 us
  blocking collectives: 17 us -> 17.9 us
    pallas_call x1, Pallas kernels: 13.1 us -> 7.95 us  [on_device(): pl.pallas_call(trunk_kernel, out_shape=(shape((rows * cu, lanes), BF16),...]
    all_to_all x1, blocking collectives: 17 us -> 17.9 us  [on_device(): lax.all_to_all(outgoing, 'gz', split_axis=0, concat_axis=0, tiled=True)]
    pallas_call x1, Pallas kernels: 2.2 us -> 1.34 us  [on_device(): pl.pallas_call(inner_kernel, out_shape=shape((2, rows + 2, 2 * cu, lanes)...]
  transfers between devices with their start and end apart: 4 -> 4, of which waited for: 0 -> 0; matrix products, arithmetic and copies ran while one was open for 8% -> 9% of each run, Pallas kernels for 5% -> 3%
where the time goes in v3:
time: 43.3 us; the launch traced here: 43 us
  blocking collectives  17.9 us (41%)
  Pallas kernels  10.6 us (24%)
  starting transfers between devices  8.51 us (20%)
  local copies, waits for them, and re-layouts  3.46 us (8%)
  other arithmetic  2.29 us (5%)
    all_to_all x1, blocking collectives, on_device(): lax.all_to_all(outgoing, 'gz', split_axis=0, concat_axis=0, tiled=True)  17.9 us
    pallas_call x1, Pallas kernels, on_device(): pl.pallas_call(trunk_kernel, out_shape=(shape((rows * cu, lanes), BF16),...  7.95 us
    ppermute x1, starting transfers between devices, on_device(): from_pair = lax.ppermute(jnp.where(odd == 1, lower, upper), 'gz', pair)  4.42 us
    ppermute x1, starting transfers between devices, on_device(): edge_pair = lax.ppermute(to_pair, 'gz', pair)  2.76 us
    unnamed x12, local copies, waits for them, and re-layouts  1.55 us
    pallas_call x1, Pallas kernels, on_device(): pl.pallas_call(inner_kernel, out_shape=shape((2, rows + 2, 2 * cu, lanes)...  1.34 us
    pallas_call x1, Pallas kernels, on_device(): pl.pallas_call(tail_kernel, out_shape=shape((devices * SEND_CAP, 3 * dept...  1.32 us
    select_n x1, other arithmetic, on_device(): from_next = lax.ppermute(jnp.where(odd == 1, upper, lower), 'gz', after)  1.16 us
  transfers between devices with their start and end apart: 4, of which 0 were waited for; matrix products, arithmetic and copies ran while one was open for 9% of the time, Pallas kernels for 3%

profile of v3, /device:TPU:0, one launch (start us, length us, event | category | flops | bytes accessed | tf_op | source)
XLA Modules:
  0.0 43.0 jit_solution(3217276001533412297)
XLA Ops:
  0.0 0.0 copy-start
  0.0 0.0 copy-start.2
  0.0 0.0 copy-start.1
  0.0 1.2 %broadcast_select_fusion = (bf16[12,3,32,128]{3,2,1,0:T(8,128)(2,1)S(1)}, bf16[12,3,32,128]{3,2,1,0:T(8,128)(2,1)S(1)}) fusion(pred[]{:T(512)S(6)} %eq.6, bf16[12,4,32,128]{3,2,1,0:T(8,128)(2,1)} %features.1), kind=kLoop, calls=%fused_computation.1 | loop fusion | flops 294912 | bytes 1179649 | tf_op jit(solution)/shard_map/jit(_where)/select_n | solution.py:341
  1.2 0.7 %collective-permute-start.1 = (bf16[12,3,32,128]{3,2,1,0:T(8,128)(2,1)S(1)}, bf16[12,3,32,128]{3,2,1,0:T(8,128)(2,1)S(1)}, u32[]{:S(2)}, u32[]{:S(2)}) collective-permute-start(bf16[12,3,32,128]{3,2,1,0:T(8,128)(2,1)S(1)} %get-tuple-element.19), channel_id=1, source_target_pairs={{1,2},{3,4},{5,6},{7,8},{9,10},{11,12},{13,14},{2,1},{4,3},{6,5},{... | collective-permute-start | bytes 884744 | tf_op jit(solution)/shard_map/ppermute | solution.py:341
  1.9 4.4 %collective-permute-start = (bf16[12,3,32,128]{3,2,1,0:T(8,128)(2,1)S(1)}, bf16[12,3,32,128]{3,2,1,0:T(8,128)(2,1)S(1)}, u32[]{:S(2)}, u32[]{:S(2)}) collective-permute-start(bf16[12,3,32,128]{3,2,1,0:T(8,128)(2,1)S(1)} %get-tuple-element.20), channel_id=1, source_target_pairs={{0,1},{1,0},{2,3},{3,2},{4,5},{5,4},{6,7},{7,6},{8,9},{9,8},{10,11... | collective-permute-start | bytes 884744 | tf_op jit(solution)/shard_map/ppermute | solution.py:342
  6.3 0.8 %broadcast_multiply_fusion = bf16[3,4,4,12]{3,2,1,0:T(4,128)(2,1)S(1)} fusion(bf16[4,4]{1,0:T(4,128)(2,1)} %constant.26.clone, bf16[3,12]{1,0:T(4,128)(2,1)} %param.14), kind=kLoop, calls=%fused_computation.18 | loop fusion | flops 576 | bytes 1256 | tf_op jit(solution)/shard_map/mul | solution.py:362
  7.1 0.1 mul.23
  7.2 0.1 tile.9
  7.2 0.9 %reshape.36 = bf16[12,3,3,144]{3,2,1,0:T(4,128)(2,1)S(1)} reshape(bf16[12,1296]{1,0:T(8,128)(2,1)} %param.13) | data formatting | bytes 62208 | tf_op jit(solution)/shard_map/reshape | solution.py:349
  8.2 0.1 pad_bitcast_fusion.2
  8.4 0.1 maximum_bitcast_fusion
  8.6 0.9 %copy.14 = bf16[48,324]{0,1:T(8,128)(2,1)S(1)} copy(bf16[48,324]{1,0:T(8,128)(2,1)} %param.10) | data formatting | bytes 62208 | tf_op args[1]
  9.6 0.0 copy-start.3
  9.6 0.0 copy-start.4
  9.6 0.1 pad_maximum_fusion
  9.7 0.2 copy.15
  9.9 0.1 reshape.35
  10.1 0.1 copy.19.w_first
  10.2 0.1 pad_add_fusion.flags
  10.3 0.0 collective-permute-done.1.from_next
  10.3 0.0 collective-permute-done.from_pair
  10.3 0.0 copy-done
  10.3 0.0 copy-done.2
  10.3 0.0 copy-done.1
  10.3 8.0 %trunk.1 = (bf16[384,128]{1,0:T(8,128)(2,1)S(1)}, bf16[384,128]{1,0:T(8,128)(2,1)S(1)}, bf16[4,32,144,128]{3,2,1,0:T(8,128)(2,1)S(1)}) custom-call(s32[3]{0:T(128)S(1)} %pad_add_fusion.flags, bf16[12,4,32,128]{3,2,1,0:T(8,128)(2,1)S(1)} %copy-done, bf16[12,3,32,128]{3,2,1,0:T(8,128)(2,1)S(1)} %collective-permute-done.from_pair, ...), custom_call_target="tpu_custom_call" | custom-call | tf_op jit(solution)/shard_map/trunk/pallas_call | solution.py:371
  18.3 2.8 %collective-permute-start.2 = (bf16[384,128]{1,0:T(8,128)(2,1)S(1)}, bf16[384,128]{1,0:T(8,128)(2,1)S(1)}, u32[]{:S(2)}, u32[]{:S(2)}) collective-permute-start(bf16[384,128]{1,0:T(8,128)(2,1)S(1)} %get-tuple-element.16), channel_id=1, source_target_pairs={{0,1},{1,0},{2,3},{3,2},{4,5},{5,4},{6,7},{7,6},{8,9},{9,8},{10,11... | collective-permute-start | bytes 294920 | tf_op jit(solution)/shard_map/ppermute | solution.py:393
  21.1 0.7 %collective-permute-start.3 = (bf16[384,128]{1,0:T(8,128)(2,1)S(1)}, bf16[384,128]{1,0:T(8,128)(2,1)S(1)}, u32[]{:S(2)}, u32[]{:S(2)}) collective-permute-start(bf16[384,128]{1,0:T(8,128)(2,1)S(1)} %get-tuple-element.17), channel_id=1, source_target_pairs={{1,2},{3,4},{5,6},{7,8},{9,10},{11,12},{13,14},{2,1},{4,3},{6,5},{... | collective-permute-start | bytes 294920 | tf_op jit(solution)/shard_map/ppermute | solution.py:392
  21.7 1.3 %inner.1 = f32[2,34,24,128]{3,2,1,0:T(8,128)S(1)} custom-call(bf16[4,32,144,128]{3,2,1,0:T(8,128)(2,1)S(1)} %get-tuple-element.14.cols_3, bf16[2,72,432]{2,1,0:T(8,128)(2,1)S(1)} %pad_maximum_fusion.1.w_inner), custom_call_target="tpu_custom_call" | custom-call | flops 509607936 | bytes 8388608 | tf_op jit(solution)/shard_map/inner/pallas_call | solution.py:394
  23.1 0.0 collective-permute-done.2.from_pair
  23.1 0.0 collective-permute-done.3.from_next
  23.1 0.0 copy-done.3
  23.1 0.0 copy-done.4
  23.1 1.3 %tail.1 = bf16[32,1536]{1,0:T(8,128)(2,1)S(1)} custom-call(s32[3]{0:T(128)S(1)} %pad_add_fusion.flags, f32[2,34,24,128]{3,2,1,0:T(8,128)S(1)} %inner.1, bf16[384,128]{1,0:T(8,128)(2,1)S(1)} %collective-permute-done.2.from_pair, bf16[384,128]{1,0:T(8,128)(2,1)S(1)} %collective-permute-done.3.from_next, bf16[16,144]{1,0:T(8,128)(2,1)S(1)} %pad.16.w_head, ...), custom_call_target="tpu_custom_call" | custom-call | tf_op jit(solution)/shard_map/tail/pallas_call | solution.py:407
  24.5 17.9 %all_to_all.5 = bf16[16,2,1536]{2,1,0:T(2,128)(2,1)S(1)} all-to-all(bf16[16,2,1536]{2,1,0:T(2,128)(2,1)S(1)} %reshape.38), channel_id=1, replica_groups=mesh['grp'=2,'gz'=16] {'gz'}, dimensions={0} | all-to-all | bytes 196608 | tf_op jit(solution)/shard_map/all_to_all | solution.py:420
  42.3 0.6 %copy.23 = bf16[1,16,2,1536]{3,2,1,0:T(2,128)(2,1)} copy(bf16[1,16,2,1536]{3,2,1,0:T(2,128)(2,1)S(1)} %bitcast.35) | data formatting | bytes 196608
  (15 shorter events, 0.3 us)
Async XLA Ops:
  0.0 10.3 %copy-start = (bf16[12,4,32,128]{3,2,1,0:T(8,128)(2,1)S(1)}, bf16[12,4,32,128]{3,2,1,0:T(8,128)(2,1)}, u32[]{:S(2)}) copy-start(bf16[12,4,32,128]{3,2,1,0:T(8,128)(2,1)} %features.1) | copy-start | bytes 1179652
  0.0 10.3 %copy-start.2 = (bf16[48,96]{1,0:T(8,128)(2,1)S(1)}, bf16[48,96]{1,0:T(8,128)(2,1)}, u32[]{:S(2)}) copy-start(bf16[48,96]{1,0:T(8,128)(2,1)} %w_lift.1) | copy-start | bytes 27652
  0.0 10.3 %copy-start.1 = (bf16[96,1296]{1,0:T(8,128)(2,1)S(1)}, bf16[96,1296]{1,0:T(8,128)(2,1)}, u32[]{:S(2)}) copy-start(bf16[96,1296]{1,0:T(8,128)(2,1)} %w_second.1) | copy-start | bytes 746500
  1.2 9.1 %collective-permute-start.1 = (bf16[12,3,32,128]{3,2,1,0:T(8,128)(2,1)S(1)}, bf16[12,3,32,128]{3,2,1,0:T(8,128)(2,1)S(1)}, u32[]{:S(2)}, u32[]{:S(2)}) collective-permute-start(bf16[12,3,32,128]{3,2,1,0:T(8,128)(2,1)S(1)} %get-tuple-element.19), channel_id=1, source_target_pairs={{1,2},{3,4},{5,6},{7,8},{9,10},{11,12},{13,14},{2,1},{4,3},{6,5},{... | collective-permute-start | bytes 884744 | tf_op jit(solution)/shard_map/ppermute | solution.py:341
  1.9 8.5 %collective-permute-start = (bf16[12,3,32,128]{3,2,1,0:T(8,128)(2,1)S(1)}, bf16[12,3,32,128]{3,2,1,0:T(8,128)(2,1)S(1)}, u32[]{:S(2)}, u32[]{:S(2)}) collective-permute-start(bf16[12,3,32,128]{3,2,1,0:T(8,128)(2,1)S(1)} %get-tuple-element.20), channel_id=1, source_target_pairs={{0,1},{1,0},{2,3},{3,2},{4,5},{5,4},{6,7},{7,6},{8,9},{9,8},{10,11... | collective-permute-start | bytes 884744 | tf_op jit(solution)/shard_map/ppermute | solution.py:342
  9.6 13.5 %copy-start.3 = (s32[1,32]{1,0:T(1,128)S(1)}, s32[1,32]{1,0:T(1,128)}, u32[]{:S(2)}) copy-start(s32[1,32]{1,0:T(1,128)} %tissue.1) | copy-start | bytes 388
  9.6 13.5 %copy-start.4 = (s32[1,32]{1,0:T(1,128)S(1)}, s32[1,32]{1,0:T(1,128)}, u32[]{:S(2)}) copy-start(s32[1,32]{1,0:T(1,128)} %owners.1) | copy-start | bytes 388
  18.3 4.8 %collective-permute-start.2 = (bf16[384,128]{1,0:T(8,128)(2,1)S(1)}, bf16[384,128]{1,0:T(8,128)(2,1)S(1)}, u32[]{:S(2)}, u32[]{:S(2)}) collective-permute-start(bf16[384,128]{1,0:T(8,128)(2,1)S(1)} %get-tuple-element.16), channel_id=1, source_target_pairs={{0,1},{1,0},{2,3},{3,2},{4,5},{5,4},{6,7},{7,6},{8,9},{9,8},{10,11... | collective-permute-start | bytes 294920 | tf_op jit(solution)/shard_map/ppermute | solution.py:393
  21.1 2.0 %collective-permute-start.3 = (bf16[384,128]{1,0:T(8,128)(2,1)S(1)}, bf16[384,128]{1,0:T(8,128)(2,1)S(1)}, u32[]{:S(2)}, u32[]{:S(2)}) collective-permute-start(bf16[384,128]{1,0:T(8,128)(2,1)S(1)} %get-tuple-element.17), channel_id=1, source_target_pairs={{1,2},{3,4},{5,6},{7,8},{9,10},{11,12},{13,14},{2,1},{4,3},{6,5},{... | collective-permute-start | bytes 294920 | tf_op jit(solution)/shard_map/ppermute | solution.py:392

commit v4 on v3

v4 whole, which is shorter than its diff:
```python
import jax
import jax.numpy as jnp
from jax import lax
from jax.experimental import pallas as pl
from jax.experimental.pallas import tpu as pltpu
from jax.sharding import PartitionSpec as P


BY = 8
BX = 16
SEND_CAP = 2
HALO = 2
F32 = jnp.float32
BF16 = jnp.bfloat16


def iota(shape, dim):
    return lax.broadcasted_iota(jnp.int32, shape, dim)


def beside(value, width):
    lane = iota(value.shape, 1) % width
    left = jnp.where(lane == 0, jnp.zeros_like(value), pltpu.roll(value, 1, 1))
    right = jnp.where(
        lane == width - 1, jnp.zeros_like(value), pltpu.roll(value, value.shape[1] - 1, 1)
    )
    return left, value, right


def neighbours():
    here = lax.axis_index("gz")
    return here % 2, here > 0, here < lax.axis_size("gz") - 1


def cut_kernel(features, *rest):
    *refs, sems = rest
    half = (len(refs) - 3) // 2
    weights, (to_pair, to_next, held), fetched = refs[:half], refs[half : half + 3], refs[half + 3 :]
    odd = lax.axis_index("gz") % 2
    depth = features.shape[1]
    top, bottom = depth - HALO, 0
    copies = [
        pltpu.make_async_copy(
            features.at[:, pl.ds(jnp.where(odd == 1, top, bottom), HALO)], to_next, sems.at[0]
        ),
        pltpu.make_async_copy(
            features.at[:, pl.ds(jnp.where(odd == 1, bottom, top), HALO)], to_pair, sems.at[1]
        ),
    ]
    for k, pair in enumerate(zip((features, *weights), (held, *fetched))):
        copies.append(pltpu.make_async_copy(*pair, sems.at[2 + k]))
    for copy in copies:
        copy.start()
    for copy in copies:
        copy.wait()


def spread(plain, cols, pitch, group, rows):
    blank = jnp.zeros((3 * group, plain.shape[1]), BF16)
    cols[0] = blank
    cols[rows + 1] = blank
    for y in range(rows):
        face = plain[pl.ds(y, group, stride=pitch), :].astype(BF16)
        cols[y + 1] = jnp.concatenate(beside(face, face.shape[1]), axis=0)


def convolve_pair(weight, cols, first, at, rows, c1):
    run = 16
    lanes = cols.shape[2]
    for y in range(0, rows, run):
        x = jnp.concatenate(
            [
                jnp.concatenate([cols[y + b + j] for b in range(3)], axis=0)
                for j in range(run)
            ],
            axis=1,
        )
        out = jnp.dot(weight, x, preferred_element_type=F32)
        out = jnp.maximum(out, 0.0).astype(BF16)
        for j in range(run):
            for z in range(2):
                first[at + z, y + j] = out[z * c1 : (z + 1) * c1, j * lanes : (j + 1) * lanes]


def crest(*faces):
    top = faces[0]
    for face in faces[1:]:
        top = jnp.maximum(top, face)
    return jnp.maximum(top, pltpu.roll(top, top.shape[1] - 1, 1))


def even_lanes(lanes):
    return (iota((2 * lanes, lanes), 0) == 2 * iota((2 * lanes, lanes), 1)).astype(BF16)


def local_kernel(w_first, features, taps, near, to_pair, to_next, plain, cols):
    c0, depth, rows, lanes = features.shape
    c1 = w_first.shape[0]
    odd, _, _ = neighbours()
    pitch = plain.shape[0] // (depth * c0)
    weight = w_first[...]
    blank = jnp.zeros((c1, c0), BF16)
    for o in range(2):
        line = []
        for b in range(3):
            for d in range(3):
                for z in range(4):
                    at = (((z - o) * 3 + b) * 3 + d) * c0
                    line.append(weight[:, at : at + c0] if 0 <= z - o < 3 else blank)
        taps[o * c1 : (o + 1) * c1] = jnp.concatenate(line, axis=1)
    for z in range(depth):
        for c in range(c0):
            at = (z * c0 + c) * pitch
            plain[at : at + rows] = features[c, z].astype(F32)
    spread(plain, cols, pitch, 4 * c0, rows)
    convolve_pair(taps[...], cols, near, 0, rows, c1)
    fold = rows // 4
    tops = []
    for z in range(2):
        for y in range(fold):
            tops.append(
                jnp.concatenate(
                    [
                        crest(near[z, 2 * k], near[z, 2 * k + 1])
                        for k in (y, y + fold)
                    ],
                    axis=1,
                )
            )
    packed = jnp.dot(
        jnp.concatenate(tops, axis=0), even_lanes(lanes), preferred_element_type=F32
    ).astype(BF16)
    for y in range(fold):
        down = packed[y * c1 : (y + 1) * c1]
        up = packed[(fold + y) * c1 : (fold + y + 1) * c1]
        to_pair[y] = jnp.where(odd == 1, down, up)
        to_next[y] = jnp.where(odd == 1, up, down)


def first_kernel(taps, features, from_pair, from_next, first, plain, cols):
    c0, depth, rows, _ = features.shape
    c1 = first.shape[2]
    odd, _, _ = neighbours()
    pitch = plain.shape[1] // (4 * c0)
    for z in range(2):
        for c in range(c0):
            at = (z * c0 + c) * pitch
            after = ((z + 2) * c0 + c) * pitch
            a = from_pair[c, z].astype(F32)
            b = from_next[c, z].astype(F32)
            plain[0, at : at + rows] = jnp.where(odd == 1, a, b)
            plain[1, after : after + rows] = jnp.where(odd == 1, b, a)
            plain[0, after : after + rows] = features[c, z].astype(F32)
            plain[1, at : at + rows] = features[c, depth - 2 + z].astype(F32)
    weight = taps[...]
    for g in range(2):
        spread(plain.at[g], cols.at[g], pitch, 4 * c0, rows)
        convolve_pair(weight, cols.at[g], first, 2 * g, rows, c1)


def trunk_kernel(
    first,
    near,
    from_pair,
    from_next,
    w_second,
    w_lift,
    w_edge,
    to_pair,
    to_next,
    cols_3,
    cols_2,
    border,
    edge,
):
    _, rows, c1, lanes = first.shape
    c2 = w_second.shape[0]
    depth = cols_3.shape[0]
    half_rows = rows // 2
    odd, low_ok, high_ok = neighbours()
    own = (first.at[1], near.at[0], near.at[1], first.at[2])

    pick = even_lanes(lanes)
    lane = iota((c1, lanes), 1)
    low_half = lane < lanes // 2
    keep_low = jnp.logical_or(jnp.logical_not(low_half), low_ok)
    keep_high = jnp.logical_or(low_half, high_ok)
    pad_2 = jnp.zeros((3 * c1, lanes), BF16)
    zero_2 = jnp.zeros((c1, lanes), BF16)
    for a in range(3):
        cols_2[a, 0] = pad_2
        cols_2[a, half_rows + 1] = pad_2
    run_p = 4
    fold = half_rows // 2
    for y0 in range(0, half_rows, run_p):
        both = []
        for k in range(y0, y0 + run_p):
            y = 2 * k
            both.append(
                jnp.concatenate(
                    [
                        crest(first[0, y], first[0, y + 1]),
                        crest(own[0][y], own[0][y + 1], own[1][y], own[1][y + 1]),
                    ],
                    axis=1,
                )
            )
            both.append(
                jnp.concatenate(
                    [
                        crest(own[2][y], own[2][y + 1], own[3][y], own[3][y + 1]),
                        crest(first[3, y], first[3, y + 1]),
                    ],
                    axis=1,
                )
            )
        packed = jnp.dot(
            jnp.concatenate(both, axis=0), pick, preferred_element_type=F32
        ).astype(BF16)
        for j in range(run_p):
            k = y0 + j
            at = 2 * j * c1
            a = from_pair[k % fold]
            b = from_next[k % fold]
            below = jnp.where(odd == 1, a, b)
            above = jnp.where(odd == 1, b, a)
            if k < fold:
                above = pltpu.roll(above, lanes // 2, 1)
            else:
                below = pltpu.roll(below, lanes // 2, 1)
            low = packed[at : at + c1]
            high = packed[at + c1 : at + 2 * c1]
            low = jnp.where(low_half, jnp.maximum(low, below), low)
            high = jnp.where(low_half, high, jnp.maximum(high, above))
            low = jnp.where(keep_low, low, zero_2)
            high = jnp.where(keep_high, high, zero_2)
            middle = pltpu.roll(jnp.where(low_half, high, low), lanes // 2, 1)
            for a, value in enumerate((low, middle, high)):
                cols_2[a, k + 1] = jnp.concatenate(beside(value, lanes // 2), axis=0)

    weight_2 = w_second[...]
    weight_l = w_lift[...]
    widen = (iota((lanes, 2 * lanes), 0) == iota((lanes, 2 * lanes), 1) // 2).astype(BF16)
    run_2 = 4

    def conv_2(i, carry):
        y = i * run_2
        x = jnp.concatenate(
            [
                jnp.concatenate(
                    [cols_2[a, y + b + j] for a in range(3) for b in range(3)], axis=0
                )
                for j in range(run_2)
            ],
            axis=1,
        )
        second = jnp.dot(weight_2, x, preferred_element_type=F32)
        second = jnp.maximum(second, 0.0).astype(BF16)
        stacked = jnp.concatenate(
            [second[:, j * lanes : (j + 1) * lanes] for j in range(run_2)], axis=0
        )
        stacked = jnp.dot(stacked, widen, preferred_element_type=F32).astype(BF16)
        spread = jnp.concatenate(
            [stacked[j * c2 : (j + 1) * c2] for j in range(run_2)], axis=1
        )
        lifted = jnp.dot(weight_l, spread, preferred_element_type=F32)
        for j in range(run_2):
            for zz in range(2):
                at = (2 * j + zz) * lanes
                value = lifted[:, at : at + lanes]
                for dz in range(2):
                    for dy in range(2):
                        z = 2 * zz + dz
                        row = 2 * (y + j) + dy
                        merged = value + own[z][row].astype(F32)
                        merged = merged.astype(BF16)
                        cols_3[z, row] = jnp.concatenate(beside(merged, lanes), axis=0)
        return carry

    lax.fori_loop(0, half_rows // run_2, conv_2, 0, unroll=4)

    cu = edge.shape[0] // rows
    border[...] = jnp.zeros_like(border)
    weight_e = w_edge[...]
    run_e = 8

    def conv_e(i, carry):
        y = i * run_e
        x = jnp.concatenate(
            [
                jnp.concatenate([cols_3[0, y + j], cols_3[depth - 1, y + j]], axis=0)
                for j in range(run_e)
            ],
            axis=1,
        )
        out = jnp.dot(weight_e, x, preferred_element_type=F32)
        for k, term in row_sums(out, run_e, 2 * cu, lanes):
            border[y + k] += term
        return carry

    lax.fori_loop(0, rows // run_e, conv_e, 0, unroll=4)

    for target, upward in ((to_pair, odd == 0), (to_next, odd == 1)):
        for y in range(rows):
            down = border[y + 1, 0:cu]
            up = border[y + 1, cu : 2 * cu]
            edge[y * cu : (y + 1) * cu] = jnp.where(upward, up, down)
        target[...] = edge[...].astype(BF16)


def weights_kernel(w_merge, w_affine, w_edge, w_inner, head):
    cu, width = w_merge.shape
    width = width // 9
    merge = w_merge[...].astype(F32)
    none = jnp.zeros((cu, width), F32)

    def arrange(table):
        lines = []
        for b in range(3):
            for line in table:
                pieces = [
                    none if a is None else merge[:, (a * 3 + b) * width : (a * 3 + b + 1) * width]
                    for a in line
                ]
                lines.append(jnp.concatenate(pieces, axis=1))
        return jnp.concatenate(lines, axis=0).astype(BF16)

    w_edge[...] = arrange([[2, None], [None, 0]])
    w_inner[0] = arrange([[1, 2, None], [0, 1, 2]])
    w_inner[1] = arrange([[None, 0, 1], [0, 1, 2]])

    affine = w_affine[...].astype(F32)
    blank = jnp.zeros_like(affine)
    lines = []
    for z in range(4):
        at = (0, 1, 3, 2).index(z)
        line = [affine if k == at else blank for k in range(4)]
        lines.append(jnp.concatenate(line * 3, axis=1))
    lines.append(jnp.zeros((16 - 4 * affine.shape[0], 12 * cu), F32))
    head[...] = jnp.concatenate(lines, axis=0).astype(BF16)


def row_sums(out, run, height, lanes):
    for k in range(run + 2):
        term = None
        for b in range(3):
            j = k - 2 + b
            if 0 <= j < run:
                value = out[b * height : (b + 1) * height, j * lanes : (j + 1) * lanes]
                term = value if term is None else term + value
        yield k, term


def inner_kernel(cols_3, w_inner, inner):
    _, rows, _, lanes = cols_3.shape
    height = inner.shape[2]
    run = 8
    for q in range(2):
        inner[q, 0] = jnp.zeros((height, lanes), F32)
        inner[q, 1] = jnp.zeros((height, lanes), F32)
        weight = w_inner[q]

        def conv_3(i, carry, q=q, weight=weight):
            y = i * run
            x = jnp.concatenate(
                [
                    jnp.concatenate([cols_3[q + a, y + j] for a in range(3)], axis=0)
                    for j in range(run)
                ],
                axis=1,
            )
            out = jnp.dot(weight, x, preferred_element_type=F32)
            for k, term in row_sums(out, run, height, lanes):
                if k < 2:
                    inner[q, y + k] += term
                else:
                    inner[q, y + k] = term
            return carry

        lax.fori_loop(0, rows // run, conv_3, 0, unroll=4)


def tail_kernel(inner, from_pair, from_next, w_head, tissue, owners, out, edge, shown):
    depth = 4
    height, lanes = inner.shape[2:]
    rows = inner.shape[1] - 2
    cu = from_pair.shape[0] // rows
    odd, _, _ = neighbours()
    a = from_pair[...].astype(F32)
    b = from_next[...].astype(F32)
    edge[0] = jnp.where(odd == 1, a, b)
    edge[1] = jnp.where(odd == 1, b, a)
    head = w_head[...]
    gap = jnp.zeros((height - cu, lanes), F32)
    run = 8
    for y0 in range(0, rows, run):
        columns = []
        for y in range(y0, y0 + run):
            parts = []
            value = jnp.concatenate(
                [
                    inner[q, y + 1]
                    + jnp.concatenate([edge[q, y * cu : (y + 1) * cu], gap], axis=0)
                    for q in range(2)
                ],
                axis=0,
            )
            value = jnp.maximum(value, 0.0)
            for _ in range(3):
                part = value.astype(BF16)
                parts.append(part)
                value = value - part.astype(F32)
            columns.append(jnp.concatenate(parts, axis=0))
        logits = jnp.dot(head, jnp.concatenate(columns, axis=1), preferred_element_type=F32)
        chance = jax.nn.sigmoid(logits)
        for j in range(run):
            shown[(y0 + j) * 24 : (y0 + j) * 24 + 16] = chance[:, j * lanes : (j + 1) * lanes]

    sub = iota((BY, lanes), 0)
    group = iota((BY, lanes), 1) // BX
    faces = 3 * depth
    tiles = []
    for f in range(faces):
        blocks = []
        line = f % depth * 3 + f // depth
        for by in range(rows // BY):
            v = shown[pl.ds(by * BY * 24 + line, BY, stride=24), :]
            for k in (1, 2, 4):
                s_bit = (sub // k) % 2
                g_bit = (group // k) % 2
                down = pltpu.roll(pltpu.roll(v, BY - k, 0), k * BX, 1)
                up = pltpu.roll(pltpu.roll(v, k, 0), lanes - k * BX, 1)
                v = jnp.where(s_bit == g_bit, v, jnp.where(s_bit < g_bit, down, up))
            blocks.append(v)
        tiles.append(jnp.concatenate(blocks, axis=0))
    tiles = jnp.concatenate(tiles, axis=1).astype(BF16)

    count = tissue.shape[1]
    slots = out.shape[0]
    own = jnp.broadcast_to(owners[...], (count, count))
    seen = jnp.broadcast_to(tissue[...], (count, count))
    r = iota((count, count), 0)
    c = iota((count, count), 1)
    own_column = jnp.sum(jnp.where(r == c, own, 0), axis=1, keepdims=True)
    seen_column = jnp.sum(jnp.where(r == c, seen, 0), axis=1, keepdims=True)
    before = jnp.where(jnp.logical_and(own_column == own, r < c), 1, 0)
    slot = owners[...] * SEND_CAP + jnp.sum(before, axis=0, keepdims=True)
    slot_pick = (iota((slots, count), 0) == slot).astype(F32).astype(BF16)
    blocks = tiles.shape[0]
    block_pick = (seen_column == iota((count, blocks), 1)).astype(F32).astype(BF16)
    select = jnp.dot(slot_pick, block_pick, preferred_element_type=F32).astype(BF16)
    out[...] = jnp.dot(select, tiles, preferred_element_type=F32).astype(BF16)


def on_device(features, w_first, w_second, w_lift, w_merge, w_affine, tissue, owners):
    c0, depth, rows, lanes = features.shape
    c1, c2 = w_lift.shape
    cu = w_merge.shape[0]
    devices = lax.axis_size("gz")
    pair = [(i, i ^ 1) for i in range(devices)]
    after = [(i, i + 1) for i in range(1, devices - 1, 2)]
    after = after + [(j, i) for i, j in after]

    def swap(to_pair, to_next):
        from_next = lax.ppermute(to_next, "gz", after)
        from_pair = lax.ppermute(to_pair, "gz", pair)
        return from_pair, from_next

    vmem = pl.BlockSpec(memory_space=pltpu.VMEM)
    shape = jax.ShapeDtypeStruct
    pitch = rows + 8
    group = 4 * c0

    def call(kernel, outs, count, scratch, mib, flops, space=vmem):
        return pl.pallas_call(
            kernel,
            out_shape=outs,
            in_specs=[space] * count,
            out_specs=jax.tree.map(lambda _: vmem, outs),
            scratch_shapes=scratch,
            compiler_params=pltpu.CompilerParams(vmem_limit_bytes=mib * 2**20),
            cost_estimate=pl.CostEstimate(
                flops=flops, bytes_accessed=4 * 2**20, transcendentals=0
            ),
        )

    halo = shape((c0, HALO, rows, lanes), BF16)
    sources = (features, w_first, w_merge, w_affine, w_second, w_lift)
    to_pair, to_next, *held = call(
        cut_kernel,
        tuple(pltpu.VMEM(a.shape, a.dtype) for a in (halo, halo, *sources)),
        len(sources),
        [pltpu.SemaphoreType.DMA((2 + len(sources),))],
        60,
        0,
        pl.BlockSpec(memory_space=pltpu.HBM),
    )(*sources)
    features, w_first, w_merge, w_affine, w_second, w_lift = held
    from_pair, from_next = swap(to_pair, to_next)

    tops = shape((rows // 4, c1, lanes), BF16)
    taps, near, tops_to_pair, tops_to_next = call(
        local_kernel,
        (shape((2 * c1, 9 * group), BF16), shape((2, rows, c1, lanes), BF16), tops, tops),
        2,
        [
            pltpu.VMEM((group * pitch, lanes), F32),
            pltpu.VMEM((rows + 2, 3 * group, lanes), BF16),
        ],
        12,
        2 * 27 * c0 * c1 * 2 * rows * lanes,
    )(w_first, features)
    tops_pair, tops_next = swap(tops_to_pair, tops_to_next)

    first = call(
        first_kernel,
        shape((4, rows, c1, lanes), BF16),
        4,
        [
            pltpu.VMEM((2, group * pitch, lanes), F32),
            pltpu.VMEM((2, rows + 2, 3 * group, lanes), BF16),
        ],
        12,
        2 * 27 * c0 * c1 * 4 * rows * lanes,
    )(taps, features, from_pair, from_next)
    w_edge, w_inner, head = call(
        weights_kernel,
        (
            shape((6 * cu, 6 * c1), BF16),
            shape((2, 6 * cu, 9 * c1), BF16),
            shape((16, 12 * cu), BF16),
        ),
        2,
        [],
        4,
        2**20,
    )(w_merge, w_affine)
    edges = shape((rows * cu, lanes), BF16)
    to_pair, to_next, cols_3 = call(
        trunk_kernel,
        (edges, edges, shape((depth, rows, 3 * c1, lanes), BF16)),
        7,
        [
            pltpu.VMEM((3, rows // 2 + 2, 3 * c1, lanes), BF16),
            pltpu.VMEM((rows + 2, 2 * cu, lanes), F32),
            pltpu.VMEM((rows * cu, lanes), F32),
        ],
        16,
        2 * 27 * c1 * c2 * depth * rows * lanes // 8,
    )(first, near, tops_pair, tops_next, w_second, w_lift, w_edge)
    edge_pair, edge_next = swap(to_pair, to_next)
    inner = call(
        inner_kernel,
        shape((2, rows + 2, 2 * cu, lanes), F32),
        2,
        [],
        16,
        2 * 27 * c1 * cu * depth * rows * lanes,
    )(cols_3, w_inner)
    outgoing = call(
        tail_kernel,
        shape((devices * SEND_CAP, 3 * depth * BY * BX), BF16),
        6,
        [
            pltpu.VMEM((2, rows * cu, lanes), F32),
            pltpu.VMEM((rows * 24, lanes), F32),
        ],
        8,
        2**20,
    )(inner, edge_pair, edge_next, head, tissue, owners)
    outgoing = outgoing.reshape(devices, SEND_CAP, -1)
    return lax.all_to_all(outgoing, "gz", split_axis=0, concat_axis=0, tiled=True)[None]


def solution(mesh):
    placed = (
        P(None, ("grp", "gz"), None, None),
        P(),
        P(),
        P(),
        P(),
        P(),
        P(("grp", "gz"), None),
        P(("grp", "gz"), None),
    )
    return jax.shard_map(
        on_device,
        mesh=mesh,
        in_specs=placed,
        out_specs=P(("grp", "gz"), None, None, None),
        check_vma=False,
    )
```

time: 43.3 us -> 39.5 us (0.912)
  local copies, waits for them, and re-layouts: 3.46 us -> 0.69 us
  other arithmetic: 2.29 us -> 0 us
  starting transfers between devices: 8.51 us -> 10.1 us
  Pallas kernels: 10.6 us -> 9.89 us
  blocking collectives: 17.9 us -> 18.4 us
    ppermute x4 -> x6, starting transfers between devices: 8.51 us -> 10.1 us  [the longest x3 8.13 us: swap(): from_pair = lax.ppermute(to_pair, 'gz', pair)]
    select_n x1 -> x0, other arithmetic: 1.16 us -> none  [on_device(): from_next = lax.ppermute(jnp.where(odd == 1, upper, lower), 'gz', after)]
    reshape x5 -> x0, local copies, waits for them, and re-layouts: 1.12 us -> none  [the longest x2 0.92 us: on_device(): merge = w_merge.reshape(cu, 3, 3, 3 * c1).transpose(1, 2, 0, 3)]
    unnamed x12 -> x5, local copies, waits for them, and re-layouts: 1.55 us -> 0.65 us
    mul x1 -> x0, other arithmetic: 0.77 us -> none  [on_device(): head = w_affine[:, None, None, :] * place[None, :, :, None]]
    pallas_call x3 -> x7, Pallas kernels: 10.6 us -> 9.89 us  [the longest x1 3.52 us: on_device(): call(trunk_kernel, (edges, edges, shape((depth, rows, 3 * c1, lanes), BF1...]
    all_to_all x1, blocking collectives: 17.9 us -> 18.4 us  [on_device(): lax.all_to_all(outgoing, 'gz', split_axis=0, concat_axis=0, tiled=True)]
    another operation x8 -> x0, local copies, waits for them, and re-layouts: 0.54 us -> none  [the longest x2 0.27 us: on_device(): jnp.stack([jnp.pad(taps, ((0, 0),) * 3 + ((z, 1 - z), (0, 0))) for z in r...]
  transfers between devices with their start and end apart: 4 -> 6, of which waited for: 0 -> 0; matrix products, arithmetic and copies ran while one was open for 9% -> 0% of each run, Pallas kernels for 3% -> 11%
where the time goes in v4:
time: 39.5 us; the launch traced here: 39.3 us
  blocking collectives  18.4 us (47%)
  starting transfers between devices  10.1 us (26%)
  Pallas kernels  9.89 us (25%)
  local copies, waits for them, and re-layouts  0.69 us (2%)
    all_to_all x1, blocking collectives, on_device(): lax.all_to_all(outgoing, 'gz', split_axis=0, concat_axis=0, tiled=True)  18.4 us
    ppermute x3, starting transfers between devices, swap(): from_pair = lax.ppermute(to_pair, 'gz', pair)  8.13 us
    pallas_call x1, Pallas kernels, on_device(): call(trunk_kernel, (edges, edges, shape((depth, rows, 3 * c1, lanes), BF1...  3.52 us
    ppermute x3, starting transfers between devices, swap(): from_next = lax.ppermute(to_next, 'gz', after)  1.97 us
    pallas_call x1, Pallas kernels, on_device(): call(first_kernel, shape((4, rows, c1, lanes), BF16), 4, [pltpu.VMEM((2,...  1.53 us
    pallas_call x1, Pallas kernels, on_device(): call(cut_kernel, tuple((pltpu.VMEM(a.shape, a.dtype) for a in (halo, halo...  1.39 us
    pallas_call x1, Pallas kernels, on_device(): call(inner_kernel, shape((2, rows + 2, 2 * cu, lanes), F32), 2, [], 16, 2...  1.35 us
    pallas_call x1, Pallas kernels, on_device(): call(local_kernel, (shape((2 * c1, 9 * group), BF16), shape((2, rows, c1,...  1.2 us
  transfers between devices with their start and end apart: 6, of which 0 were waited for; matrix products, arithmetic and copies ran while one was open for 0% of the time, Pallas kernels for 11%

profile of v4, /device:TPU:0, one launch (start us, length us, event | category | flops | bytes accessed | tf_op | source)
XLA Modules:
  0.0 39.3 jit_solution(11585531507488068954)
XLA Ops:
  0.0 1.4 %shard_map.82 = (bf16[12,2,32,128]{3,2,1,0:T(8,128)(2,1)S(1)}, bf16[12,2,32,128]{3,2,1,0:T(8,128)(2,1)S(1)}, bf16[12,4,32,128]{3,2,1,0:T(8,128)(2,1)S(1)}, bf16[...) custom-call(bf16[12,4,32,128]{3,2,1,0:T(8,128)(2,1)} %features.1, ...), custom_call_target="tpu_custom_call" | custom-call | bytes 4194304 | tf_op jit(solution)/shard_map/pallas_call | solution.py:489
  1.4 0.6 %collective-permute-start = (bf16[12,2,32,128]{3,2,1,0:T(8,128)(2,1)S(1)}, bf16[12,2,32,128]{3,2,1,0:T(8,128)(2,1)S(1)}, u32[]{:S(2)}, u32[]{:S(2)}) collective-permute-start(bf16[12,2,32,128]{3,2,1,0:T(8,128)(2,1)S(1)} %get-tuple-element.26), channel_id=1, source_target_pairs={{0,1},{1,0},{2,3},{3,2},{4,5},{5,4},{6,7},{7,6},{8,9},{9,8},{10,11... | collective-permute-start | bytes 589832 | tf_op jit(solution)/shard_map/ppermute | solution.py:466
  2.0 0.7 %collective-permute-start.1 = (bf16[12,2,32,128]{3,2,1,0:T(8,128)(2,1)S(1)}, bf16[12,2,32,128]{3,2,1,0:T(8,128)(2,1)S(1)}, u32[]{:S(2)}, u32[]{:S(2)}) collective-permute-start(bf16[12,2,32,128]{3,2,1,0:T(8,128)(2,1)S(1)} %get-tuple-element.27), channel_id=1, source_target_pairs={{1,2},{3,4},{5,6},{7,8},{9,10},{11,12},{13,14},{2,1},{4,3},{6,5},{... | collective-permute-start | bytes 589832 | tf_op jit(solution)/shard_map/ppermute | solution.py:465
  2.6 1.2 %shard_map.83 = (bf16[96,432]{1,0:T(8,128)(2,1)S(1)}, bf16[2,32,48,128]{3,2,1,0:T(8,128)(2,1)S(1)}, bf16[8,48,128]{2,1,0:T(8,128)(2,1)S(1)}, bf16[8,48,128]{2,1,0:T(8,128)(2,1)S(1)}) custom-call(bf16[48,324]{1,0:T(8,128)(2,1)S(1)} %get-tuple-element.23.w_first, bf16[12,4,32,128]{3,2,1,0:T(8,128)(2,1)S(1)} %get-tuple-element.24.features), custom_call_target="tpu_custom_call" | custom-call | flops 254803968 | bytes 4194304 | tf_op jit(solution)/shard_map/pallas_call | solution.py:502
  3.8 3.9 %collective-permute-start.2 = (bf16[8,48,128]{2,1,0:T(8,128)(2,1)S(1)}, bf16[8,48,128]{2,1,0:T(8,128)(2,1)S(1)}, u32[]{:S(2)}, u32[]{:S(2)}) collective-permute-start(bf16[8,48,128]{2,1,0:T(8,128)(2,1)S(1)} %get-tuple-element.29), channel_id=1, source_target_pairs={{0,1},{1,0},{2,3},{3,2},{4,5},{5,4},{6,7},{7,6},{8,9},{9,8},{10,11... | collective-permute-start | bytes 294920 | tf_op jit(solution)/shard_map/ppermute | solution.py:466
  7.8 0.7 %collective-permute-start.3 = (bf16[8,48,128]{2,1,0:T(8,128)(2,1)S(1)}, bf16[8,48,128]{2,1,0:T(8,128)(2,1)S(1)}, u32[]{:S(2)}, u32[]{:S(2)}) collective-permute-start(bf16[8,48,128]{2,1,0:T(8,128)(2,1)S(1)} %get-tuple-element.30), channel_id=1, source_target_pairs={{1,2},{3,4},{5,6},{7,8},{9,10},{11,12},{13,14},{2,1},{4,3},{6,5},{... | collective-permute-start | bytes 294920 | tf_op jit(solution)/shard_map/ppermute | solution.py:465
  8.4 0.1 shard_map.85
  8.6 0.0 collective-permute-done.from_pair
  8.6 0.0 collective-permute-done.1.from_next
  8.6 1.5 %shard_map.84.first = bf16[4,32,48,128]{3,2,1,0:T(8,128)(2,1)S(1)} custom-call(bf16[96,432]{1,0:T(8,128)(2,1)S(1)} %get-tuple-element.25.taps, bf16[12,4,32,128]{3,2,1,0:T(8,128)(2,1)S(1)} %get-tuple-element.24.features, bf16[12,2,32,128]{3,2,1,0:T(8,128)(2,1)S(1)} %collective-permute-done.from_pair, ...), custom_call_target="tpu_custom_call" | custom-call | flops 509607936 | bytes 4194304 | tf_op jit(solution)/shard_map/pallas_call | solution.py:515
  10.1 0.0 copy-start
  10.1 0.0 copy-start.1
  10.1 0.0 collective-permute-done.2.from_pair
  10.1 0.0 collective-permute-done.3.from_next
  10.2 3.5 %shard_map.86 = (bf16[384,128]{1,0:T(8,128)(2,1)S(1)}, bf16[384,128]{1,0:T(8,128)(2,1)S(1)}, bf16[4,32,144,128]{3,2,1,0:T(8,128)(2,1)S(1)}) custom-call(bf16[4,32,48,128]{3,2,1,0:T(8,128)(2,1)S(1)} %shard_map.84.first, bf16[2,32,48,128]{3,2,1,0:T(8,128)(2,1)S(1)} %get-tuple-element.28.near, bf16[8,48,128]{2,1,0:T(8,128)(2,1)S(1)} %collective-permute-done.2.from_pair, ...), custom_call_target="tpu_custom_call" | custom-call | flops 509607936 | bytes 4194304 | tf_op jit(solution)/shard_map/pallas_call | solution.py:539
  13.7 3.6 %collective-permute-start.4 = (bf16[384,128]{1,0:T(8,128)(2,1)S(1)}, bf16[384,128]{1,0:T(8,128)(2,1)S(1)}, u32[]{:S(2)}, u32[]{:S(2)}) collective-permute-start(bf16[384,128]{1,0:T(8,128)(2,1)S(1)} %get-tuple-element.38), channel_id=1, source_target_pairs={{0,1},{1,0},{2,3},{3,2},{4,5},{5,4},{6,7},{7,6},{8,9},{9,8},{10,11... | collective-permute-start | bytes 294920 | tf_op jit(solution)/shard_map/ppermute | solution.py:466
  17.3 0.7 %collective-permute-start.5 = (bf16[384,128]{1,0:T(8,128)(2,1)S(1)}, bf16[384,128]{1,0:T(8,128)(2,1)S(1)}, u32[]{:S(2)}, u32[]{:S(2)}) collective-permute-start(bf16[384,128]{1,0:T(8,128)(2,1)S(1)} %get-tuple-element.39), channel_id=1, source_target_pairs={{1,2},{3,4},{5,6},{7,8},{9,10},{11,12},{13,14},{2,1},{4,3},{6,5},{... | collective-permute-start | bytes 294920 | tf_op jit(solution)/shard_map/ppermute | solution.py:465
  18.0 1.4 %shard_map.87.inner = f32[2,34,24,128]{3,2,1,0:T(8,128)S(1)} custom-call(bf16[4,32,144,128]{3,2,1,0:T(8,128)(2,1)S(1)} %get-tuple-element.36.cols_3, bf16[2,72,432]{2,1,0:T(8,128)(2,1)S(1)} %get-tuple-element.37.w_inner), custom_call_target="tpu_custom_call" | custom-call | flops 509607936 | bytes 4194304 | tf_op jit(solution)/shard_map/pallas_call | solution.py:552
  19.3 0.0 collective-permute-done.4.from_pair
  19.3 0.0 collective-permute-done.5.from_next
  19.3 0.0 copy-done
  19.4 0.0 copy-done.1
  19.4 0.8 %shard_map.88 = bf16[32,1536]{1,0:T(8,128)(2,1)S(1)} custom-call(f32[2,34,24,128]{3,2,1,0:T(8,128)S(1)} %shard_map.87.inner, bf16[384,128]{1,0:T(8,128)(2,1)S(1)} %collective-permute-done.4.from_pair, bf16[384,128]{1,0:T(8,128)(2,1)S(1)} %collective-permute-done.5.from_next, bf16[16,144]{1,0:T(8,128)(2,1)S(1)} %get-tuple-element.40.w_head, ...), custom_call_target="tpu_custom_call" | custom-call | flops 1048576 | bytes 4194304 | tf_op jit(solution)/shard_map/pallas_call | solution.py:560
  20.2 18.4 %all_to_all.5 = bf16[16,2,1536]{2,1,0:T(2,128)(2,1)S(1)} all-to-all(bf16[16,2,1536]{2,1,0:T(2,128)(2,1)S(1)} %reshape.3), channel_id=1, replica_groups=mesh['grp'=2,'gz'=16] {'gz'}, dimensions={0} | all-to-all | bytes 196608 | tf_op jit(solution)/shard_map/all_to_all | solution.py:572
  38.6 0.6 %copy.10 = bf16[1,16,2,1536]{3,2,1,0:T(2,128)(2,1)} copy(bf16[1,16,2,1536]{3,2,1,0:T(2,128)(2,1)S(1)} %bitcast.1) | data formatting | bytes 196608
  (1 shorter events, 0.0 us)
Async XLA Ops:
  1.4 7.2 %collective-permute-start = (bf16[12,2,32,128]{3,2,1,0:T(8,128)(2,1)S(1)}, bf16[12,2,32,128]{3,2,1,0:T(8,128)(2,1)S(1)}, u32[]{:S(2)}, u32[]{:S(2)}) collective-permute-start(bf16[12,2,32,128]{3,2,1,0:T(8,128)(2,1)S(1)} %get-tuple-element.26), channel_id=1, source_target_pairs={{0,1},{1,0},{2,3},{3,2},{4,5},{5,4},{6,7},{7,6},{8,9},{9,8},{10,11... | collective-permute-start | bytes 589832 | tf_op jit(solution)/shard_map/ppermute | solution.py:466
  2.0 6.6 %collective-permute-start.1 = (bf16[12,2,32,128]{3,2,1,0:T(8,128)(2,1)S(1)}, bf16[12,2,32,128]{3,2,1,0:T(8,128)(2,1)S(1)}, u32[]{:S(2)}, u32[]{:S(2)}) collective-permute-start(bf16[12,2,32,128]{3,2,1,0:T(8,128)(2,1)S(1)} %get-tuple-element.27), channel_id=1, source_target_pairs={{1,2},{3,4},{5,6},{7,8},{9,10},{11,12},{13,14},{2,1},{4,3},{6,5},{... | collective-permute-start | bytes 589832 | tf_op jit(solution)/shard_map/ppermute | solution.py:465
  3.8 6.3 %collective-permute-start.2 = (bf16[8,48,128]{2,1,0:T(8,128)(2,1)S(1)}, bf16[8,48,128]{2,1,0:T(8,128)(2,1)S(1)}, u32[]{:S(2)}, u32[]{:S(2)}) collective-permute-start(bf16[8,48,128]{2,1,0:T(8,128)(2,1)S(1)} %get-tuple-element.29), channel_id=1, source_target_pairs={{0,1},{1,0},{2,3},{3,2},{4,5},{5,4},{6,7},{7,6},{8,9},{9,8},{10,11... | collective-permute-start | bytes 294920 | tf_op jit(solution)/shard_map/ppermute | solution.py:466
  7.8 2.4 %collective-permute-start.3 = (bf16[8,48,128]{2,1,0:T(8,128)(2,1)S(1)}, bf16[8,48,128]{2,1,0:T(8,128)(2,1)S(1)}, u32[]{:S(2)}, u32[]{:S(2)}) collective-permute-start(bf16[8,48,128]{2,1,0:T(8,128)(2,1)S(1)} %get-tuple-element.30), channel_id=1, source_target_pairs={{1,2},{3,4},{5,6},{7,8},{9,10},{11,12},{13,14},{2,1},{4,3},{6,5},{... | collective-permute-start | bytes 294920 | tf_op jit(solution)/shard_map/ppermute | solution.py:465
  10.1 9.2 %copy-start = (s32[1,32]{1,0:T(1,128)S(1)}, s32[1,32]{1,0:T(1,128)}, u32[]{:S(2)}) copy-start(s32[1,32]{1,0:T(1,128)} %tissue.1) | copy-start | bytes 388
  10.1 9.2 %copy-start.1 = (s32[1,32]{1,0:T(1,128)S(1)}, s32[1,32]{1,0:T(1,128)}, u32[]{:S(2)}) copy-start(s32[1,32]{1,0:T(1,128)} %owners.1) | copy-start | bytes 388
  13.7 5.6 %collective-permute-start.4 = (bf16[384,128]{1,0:T(8,128)(2,1)S(1)}, bf16[384,128]{1,0:T(8,128)(2,1)S(1)}, u32[]{:S(2)}, u32[]{:S(2)}) collective-permute-start(bf16[384,128]{1,0:T(8,128)(2,1)S(1)} %get-tuple-element.38), channel_id=1, source_target_pairs={{0,1},{1,0},{2,3},{3,2},{4,5},{5,4},{6,7},{7,6},{8,9},{9,8},{10,11... | collective-permute-start | bytes 294920 | tf_op jit(solution)/shard_map/ppermute | solution.py:466
  17.3 2.0 %collective-permute-start.5 = (bf16[384,128]{1,0:T(8,128)(2,1)S(1)}, bf16[384,128]{1,0:T(8,128)(2,1)S(1)}, u32[]{:S(2)}, u32[]{:S(2)}) collective-permute-start(bf16[384,128]{1,0:T(8,128)(2,1)S(1)} %get-tuple-element.39), channel_id=1, source_target_pairs={{1,2},{3,4},{5,6},{7,8},{9,10},{11,12},{13,14},{2,1},{4,3},{6,5},{... | collective-permute-start | bytes 294920 | tf_op jit(solution)/shard_map/ppermute | solution.py:465
